TPU v7x, 32 devices: a whole 2x2x4 slice. The times are simulated.
32 devices in a mesh: dp: 4 (over y, x), expert: 8 (over z, core).
Axes of the slice: x: 2, y: 2, z: 4, core: 2. Of those that a mesh axis runs over, the one named last changes fastest.
Arguments:
- tokens: bfloat16 [4096, 2048], P(('dp', 'expert')), may hold values from -6 to 6
- cotangent: bfloat16 [4096, 2048], P(('dp', 'expert')), may hold values from -6 to 6
- prefix: int32 [4], P('dp'), may hold values from 128 to 511
- routes: int32 [4096, 6], P(('dp', 'expert')), may hold values from 0 to 15, all different within a row; in each aligned block of 128 rows (0 to 127, 128 to 255, ...) at most 72 rows name the same one
- norm1_gain: bfloat16 [2048], P('expert'), may hold values from 0.25 to 1.75
- w_query: bfloat16 [2048, 3072], P('expert'), may hold values from -0.1875 to 0.1875
- w_kv_down: bfloat16 [2048, 576], P('expert'), may hold values from -0.125 to 0.125
- kv_gain: bfloat16 [512], P('expert'), may hold values from 0.25 to 1.75
- w_kv_up: bfloat16 [512, 4096], P('expert'), may hold values from -0.25 to 0.25
- w_out: bfloat16 [2048, 2048], P('expert'), may hold values from -1 to 1
- norm2_gain: bfloat16 [2048], P('expert'), may hold values from 0.25 to 1.75
- w_router: bfloat16 [2048, 16], P('expert'), may hold values from -0.0625 to 0.0625
- shared_in: bfloat16 [2048, 5632], P('expert'), may hold values from -0.125 to 0.125
- shared_out: bfloat16 [2816, 2048], P('expert'), may hold values from -0.109375 to 0.109375
- expert_in: bfloat16 [16, 2048, 2816], P('expert', 'dp'), may hold values from -0.125 to 0.125
- expert_out: bfloat16 [16, 1408, 2048], P('expert', None, 'dp'), may hold values from -6 to 6
Outputs:
- out: bfloat16 [4096, 2048], P(('dp', 'expert'))
- grad_tokens: float32 [4096, 2048], P(('dp', 'expert'))
- grad_norm1_gain: float32 [2048], P('expert')
- grad_w_query: float32 [2048, 3072], P('expert')
- grad_w_kv_down: float32 [2048, 576], P('expert')
- grad_kv_gain: float32 [512], P('expert')
- grad_w_kv_up: float32 [512, 4096], P('expert')
- grad_w_out: float32 [2048, 2048], P('expert')
- grad_norm2_gain: float32 [2048], P('expert')
- grad_w_router: float32 [2048, 16], P('expert')
- grad_shared_in: float32 [2048, 5632], P('expert')
- grad_shared_out: float32 [2816, 2048], P('expert')
- grad_expert_in: float32 [16, 2048, 2816], P('expert', 'dp')
- grad_expert_out: float32 [16, 1408, 2048], P('expert', None, 'dp')
Inputs may be any that keep to these rules, and one draw needn't show every extreme that they name: `routes`: each row names 6 different experts. Among the rows of one device no expert is named by more than 72 rows, a bound that some block reaches of them.
All inputs are finite; a program needn't handle non-finite values.
Results may differ from a plain program's by a relative error of at most 0.029.
Values may be sent and summed in bfloat16 or wider, within the bound.
No kernel may reach another device: no remote copies, remote signals or barrier semaphores. Data moves between devices by JAX's collectives and lax.ppermute only.
A program may use at most 448 MiB of HBM per device.

v0:
```python
import jax
import jax.numpy as jnp
from jax import lax
from jax.sharding import PartitionSpec as P

D = 2048
H = 16
DN = 128
DR = 64
DV = 128
KVR = 512


EPSILON = 1e-06
MASKED = -1e30


def rms_norm(values, gain_vector):
    return (
        values
        * lax.rsqrt(jnp.mean(values * values, axis=-1, keepdims=True) + EPSILON)
        * gain_vector
    )


def tables(positions, half_width):
    frequency = 10000.0 ** (-jnp.arange(half_width, dtype=jnp.float32) / half_width)
    angles = positions.astype(jnp.float32)[:, None] * frequency[None, :]
    return (jnp.cos(angles), jnp.sin(angles))


def rotate(values, cosine, sine_table):
    half_width = values.shape[-1] // 2
    front_part = values[..., :half_width]
    back_part = values[..., half_width:]
    return jnp.concatenate(
        [
            front_part * cosine - back_part * sine_table,
            back_part * cosine + front_part * sine_table,
        ],
        axis=-1,
    )


def swiglu(joined):
    half_width = joined.shape[-1] // 2
    return jax.nn.silu(joined[..., :half_width]) * joined[..., half_width:]


def matmul(left_side, right_side):
    return jnp.dot(left_side, right_side, preferred_element_type=jnp.float32)


def matmul_tn(left_side, right_side):
    return lax.dot_general(
        left_side, right_side, (((0,), (0,)), ((), ())), preferred_element_type=jnp.float32
    )


def matmul_nt(left_side, right_side):
    return lax.dot_general(
        left_side, right_side, (((1,), (1,)), ((), ())), preferred_element_type=jnp.float32
    )


def masked_scores(
    query_nope, query_rope, key_nope, key_rope, key_start, query_pos, prefix_end, score_scale
):
    front_part = jnp.einsum(
        "qhd,khd->hqk", query_nope, key_nope, preferred_element_type=jnp.float32
    )
    back_part = jnp.einsum("qhd,kd->hqk", query_rope, key_rope, preferred_element_type=jnp.float32)
    raw_scores = (front_part + back_part) * score_scale
    key_pos = key_start + jnp.arange(key_nope.shape[0], dtype=jnp.int32)
    seen = (key_pos[None, :] <= query_pos[:, None]) | (key_pos[None, :] < prefix_end)
    return jnp.where(seen[None], raw_scores, MASKED)


def needed_block(key_start, query_pos, prefix_end):
    return (key_start <= query_pos[-1]) | (key_start < prefix_end)


def attend_stats(query_nope, query_rope, key_blocks, query_pos, prefix_end, score_scale):
    row_count = query_nope.shape[0]
    nope_blocks, value_blocks, rope_blocks, block_starts = key_blocks

    def block_step(running, block_item):
        key_nope, key_rope, key_start = block_item

        def compute_block(current):
            running_top, running_sum = current
            block_scores = masked_scores(
                query_nope,
                query_rope,
                key_nope,
                key_rope,
                key_start,
                query_pos,
                prefix_end,
                score_scale,
            )
            new_top = jnp.maximum(running_top, jnp.max(block_scores, axis=-1))
            new_sum = running_sum * jnp.exp(running_top - new_top) + jnp.sum(
                jnp.exp(block_scores - new_top[..., None]), axis=-1
            )
            return (new_top, new_sum)

        def skip_block(current):
            return current

        return (
            lax.cond(
                needed_block(key_start, query_pos, prefix_end), compute_block, skip_block, running
            ),
            None,
        )

    initial = (
        jnp.full((H, row_count), MASKED, jnp.float32),
        jnp.zeros((H, row_count), jnp.float32),
    )
    (final_top, final_sum), _ = lax.scan(
        block_step, initial, (nope_blocks, rope_blocks, block_starts)
    )
    return final_top + jnp.log(final_sum)


def attend_values(
    query_nope, query_rope, key_blocks, query_pos, prefix_end, score_scale, log_total
):
    row_count = query_nope.shape[0]

    def block_step(running, block_item):
        key_nope, key_value, key_rope, key_start = block_item

        def compute_block(current):
            block_scores = masked_scores(
                query_nope,
                query_rope,
                key_nope,
                key_rope,
                key_start,
                query_pos,
                prefix_end,
                score_scale,
            )
            weights = jnp.exp(block_scores - log_total[..., None]).astype(jnp.bfloat16)
            return current + jnp.einsum(
                "hqk,khd->qhd", weights, key_value, preferred_element_type=jnp.float32
            )

        def skip_block(current):
            return current

        return (
            lax.cond(
                needed_block(key_start, query_pos, prefix_end), compute_block, skip_block, running
            ),
            None,
        )

    initial = jnp.zeros((row_count, H, DV), jnp.float32)
    result, _ = lax.scan(block_step, initial, key_blocks)
    return result


def attend_grads(
    query_nope,
    query_rope,
    key_blocks,
    query_pos,
    prefix_end,
    score_scale,
    log_total,
    grad_out,
    row_delta,
):
    row_count = query_nope.shape[0]
    key_span = key_blocks[0].shape[1]

    def block_step(running, block_item):
        key_nope, key_value, key_rope, key_start = block_item

        def compute_block(current):
            grad_nope, grad_rope = current
            block_scores = masked_scores(
                query_nope,
                query_rope,
                key_nope,
                key_rope,
                key_start,
                query_pos,
                prefix_end,
                score_scale,
            )
            attn_probs = jnp.exp(block_scores - log_total[..., None])
            prob_grad = jnp.einsum(
                "qhd,khd->hqk", grad_out, key_value, preferred_element_type=jnp.float32
            )
            dscore = (attn_probs * (prob_grad - row_delta[..., None])).astype(jnp.bfloat16)
            grad_nope = grad_nope + score_scale * jnp.einsum(
                "hqk,khd->qhd", dscore, key_nope, preferred_element_type=jnp.float32
            )
            grad_rope = grad_rope + score_scale * jnp.einsum(
                "hqk,kd->qhd", dscore, key_rope, preferred_element_type=jnp.float32
            )
            key_grad = score_scale * jnp.einsum(
                "hqk,qhd->khd", dscore, query_nope, preferred_element_type=jnp.float32
            )
            rope_grad = score_scale * jnp.einsum(
                "hqk,qhd->kd", dscore, query_rope, preferred_element_type=jnp.float32
            )
            value_grad = jnp.einsum(
                "hqk,qhd->khd",
                attn_probs.astype(jnp.bfloat16),
                grad_out,
                preferred_element_type=jnp.float32,
            )
            return ((grad_nope, grad_rope), (key_grad, value_grad, rope_grad))

        def skip_block(current):
            empty_terms = (
                jnp.zeros((key_span, H, DN), jnp.float32),
                jnp.zeros((key_span, H, DV), jnp.float32),
                jnp.zeros((key_span, DR), jnp.float32),
            )
            return (current, empty_terms)

        return lax.cond(
            needed_block(key_start, query_pos, prefix_end), compute_block, skip_block, running
        )

    initial = (
        jnp.zeros((row_count, H, DN), jnp.float32),
        jnp.zeros((row_count, H, DR), jnp.float32),
    )
    return lax.scan(block_step, initial, key_blocks)


def split_blocks(key_parts, key_span):
    nope_all, value_all, rope_all = key_parts
    block_count = nope_all.shape[0] // key_span
    block_starts = jnp.arange(block_count, dtype=jnp.int32) * key_span
    return (
        nope_all.reshape(block_count, key_span, H, DN),
        value_all.reshape(block_count, key_span, H, DV),
        rope_all.reshape(block_count, key_span, DR),
        block_starts,
    )


def body(
    tokens,
    cotangent,
    prefix,
    routes,
    norm1_gain,
    w_query,
    w_kv_down,
    kv_gain,
    w_kv_up,
    w_out,
    norm2_gain,
    w_router,
    shared_in,
    shared_out,
    expert_in,
    expert_out,
):
    row_count = tokens.shape[0]
    topk_count = routes.shape[1]
    groups = lax.axis_size("expert")
    owned = expert_in.shape[0]
    expert_count = owned * groups
    capacity = 3 * row_count * topk_count // (2 * expert_count)
    score_scale = float(DN + DR) ** (-0.5)
    my_index = lax.axis_index("expert")
    query_pos = my_index * row_count + jnp.arange(row_count, dtype=jnp.int32)
    prefix_end = prefix[0]
    cosine, sine_table = tables(query_pos, DR // 2)
    key_span = 4 * row_count
    mixer_parts = (
        lax.all_gather(norm1_gain, "expert", axis=0, tiled=True),
        lax.all_gather(w_query, "expert", axis=0, tiled=True),
        lax.all_gather(w_kv_down, "expert", axis=0, tiled=True),
        lax.all_gather(kv_gain, "expert", axis=0, tiled=True),
        lax.all_gather(w_kv_up, "expert", axis=0, tiled=True),
        lax.all_gather(w_out, "expert", axis=0, tiled=True),
        lax.all_gather(norm2_gain, "expert", axis=0, tiled=True),
        lax.all_gather(w_router, "expert", axis=0, tiled=True),
        lax.all_gather(shared_in, "expert", axis=0, tiled=True),
        lax.all_gather(shared_out, "expert", axis=0, tiled=True),
    )
    (
        gain_one,
        query_w,
        kv_down_w,
        kv_gain_w,
        kv_up_w,
        out_w,
        gain_two,
        router_w,
        shared_in_w,
        shared_out_w,
    ) = mixer_parts
    values = tokens.astype(jnp.float32)
    normed = rms_norm(values, gain_one.astype(jnp.float32))
    normed_b = normed.astype(jnp.bfloat16)
    query_raw = matmul(normed_b, query_w).reshape(row_count, H, DN + DR)
    query_nope = query_raw[..., :DN].astype(jnp.bfloat16)
    query_rope = rotate(query_raw[..., DN:], cosine[:, None, :], sine_table[:, None, :]).astype(
        jnp.bfloat16
    )
    kv_down = matmul(normed_b, kv_down_w)
    latent = kv_down[:, :KVR]
    latent_b = rms_norm(latent, kv_gain_w.astype(jnp.float32)).astype(jnp.bfloat16)
    key_rope_b = rotate(kv_down[:, KVR:], cosine, sine_table).astype(jnp.bfloat16)
    kv_up = matmul(latent_b, kv_up_w).astype(jnp.bfloat16).reshape(row_count, H, DN + DV)
    local_nope = kv_up[..., :DN].reshape(row_count, H * DN)
    local_value = kv_up[..., DN:].reshape(row_count, H * DV)
    key_parts = (
        lax.all_gather(local_nope, "expert", axis=0, tiled=True),
        lax.all_gather(local_value, "expert", axis=0, tiled=True),
        lax.all_gather(key_rope_b, "expert", axis=0, tiled=True),
    )
    key_blocks = split_blocks(key_parts, key_span)
    log_total = attend_stats(query_nope, query_rope, key_blocks, query_pos, prefix_end, score_scale)
    attn_full = attend_values(
        query_nope, query_rope, key_blocks, query_pos, prefix_end, score_scale, log_total
    )
    mixed_b = attn_full.astype(jnp.bfloat16).reshape(row_count, H * DV)
    middle = values + matmul(mixed_b, out_w)
    gain_two_f = gain_two.astype(jnp.float32)
    normed_two_b = rms_norm(middle, gain_two_f).astype(jnp.bfloat16)
    router_probs = jax.nn.softmax(matmul(normed_two_b, router_w), axis=-1)
    one_hot = routes[:, :, None] == jnp.arange(expert_count, dtype=jnp.int32)[None, None, :]
    route_gates = jnp.sum(jnp.where(one_hot, router_probs[:, None, :], 0.0), axis=-1)
    shared_join = matmul(normed_two_b, shared_in_w)
    shared_hidden_b = swiglu(shared_join).astype(jnp.bfloat16)
    shared = matmul(shared_hidden_b, shared_out_w)
    expert_ids = routes.reshape(-1)
    id_hot = (expert_ids[:, None] == jnp.arange(expert_count, dtype=jnp.int32)[None, :]).astype(
        jnp.int32
    )
    slot_index = jnp.sum((jnp.cumsum(id_hot, axis=0) - id_hot) * id_hot, axis=1)
    slot_place = (expert_ids % owned * groups + expert_ids // owned) * capacity + slot_index
    buffer_rows = owned * groups * capacity
    filled = (
        jnp.zeros((buffer_rows, D), jnp.bfloat16)
        .at[slot_place]
        .set(jnp.repeat(normed_two_b, topk_count, axis=0))
    )
    received = lax.all_to_all(
        filled.reshape(owned, groups, capacity, D),
        "expert",
        split_axis=1,
        concat_axis=1,
        tiled=True,
    )
    expert_rows = received.reshape(owned, groups * capacity, D)
    expert_parts = (
        lax.all_gather(expert_in, "dp", axis=1, tiled=True),
        lax.all_gather(expert_out, "dp", axis=2, tiled=True),
    )
    first_w, second_w = expert_parts
    joined = jnp.einsum("erd,edf->erf", expert_rows, first_w, preferred_element_type=jnp.float32)
    hidden_b = swiglu(joined).astype(jnp.bfloat16)
    result_b = jnp.einsum(
        "erf,efd->erd", hidden_b, second_w, preferred_element_type=jnp.float32
    ).astype(jnp.bfloat16)
    returned = lax.all_to_all(
        result_b.reshape(owned, groups, capacity, D),
        "expert",
        split_axis=1,
        concat_axis=1,
        tiled=True,
    )
    picked = (
        returned.reshape(buffer_rows, D)[slot_place]
        .reshape(row_count, topk_count, D)
        .astype(jnp.float32)
    )
    routed = jnp.sum(route_gates[:, :, None] * picked, axis=1)
    out = (middle + shared + routed).astype(jnp.bfloat16)
    back_parts = (
        lax.all_gather(norm1_gain, "expert", axis=0, tiled=True),
        lax.all_gather(w_query, "expert", axis=0, tiled=True),
        lax.all_gather(w_kv_down, "expert", axis=0, tiled=True),
        lax.all_gather(kv_gain, "expert", axis=0, tiled=True),
        lax.all_gather(w_kv_up, "expert", axis=0, tiled=True),
        lax.all_gather(w_out, "expert", axis=0, tiled=True),
        lax.all_gather(norm2_gain, "expert", axis=0, tiled=True),
        lax.all_gather(w_router, "expert", axis=0, tiled=True),
        lax.all_gather(shared_in, "expert", axis=0, tiled=True),
        lax.all_gather(shared_out, "expert", axis=0, tiled=True),
    )
    back_keys = (
        lax.all_gather(local_nope, "expert", axis=0, tiled=True),
        lax.all_gather(local_value, "expert", axis=0, tiled=True),
        lax.all_gather(key_rope_b, "expert", axis=0, tiled=True),
    )
    back_blocks = split_blocks(back_keys, key_span)
    (
        gain_one_back,
        query_back,
        kv_down_back,
        kv_gain_back,
        kv_up_back,
        out_back,
        gain_two_back,
        router_back,
        shared_in_back,
        shared_out_back,
    ) = back_parts
    out_grad = cotangent.astype(jnp.float32)
    gate_grad = jnp.sum(out_grad[:, None, :] * picked, axis=2)
    result_grad = (route_gates[:, :, None] * out_grad[:, None, :]).astype(jnp.bfloat16)
    sent = jnp.zeros((buffer_rows, D), jnp.bfloat16).at[slot_place].set(result_grad.reshape(-1, D))
    owner_grad = lax.all_to_all(
        sent.reshape(owned, groups, capacity, D), "expert", split_axis=1, concat_axis=1, tiled=True
    ).reshape(owned, groups * capacity, D)
    hidden_grad = jnp.einsum(
        "erd,efd->erf", owner_grad, second_w, preferred_element_type=jnp.float32
    )
    _, pull_expert = jax.vjp(swiglu, joined)
    joined_grad = pull_expert(hidden_grad)[0].astype(jnp.bfloat16)
    grad_second = jnp.einsum(
        "erf,erd->efd", hidden_b, owner_grad, preferred_element_type=jnp.float32
    )
    grad_first = jnp.einsum(
        "erd,erf->edf", expert_rows, joined_grad, preferred_element_type=jnp.float32
    )
    rows_grad = jnp.einsum("erf,edf->erd", joined_grad, first_w, preferred_element_type=jnp.float32)
    sent_back = lax.all_to_all(
        rows_grad.reshape(owned, groups, capacity, D).astype(jnp.bfloat16),
        "expert",
        split_axis=1,
        concat_axis=1,
        tiled=True,
    ).astype(jnp.float32)
    route_grad = jnp.sum(
        sent_back.reshape(buffer_rows, D)[slot_place].reshape(row_count, topk_count, D), axis=1
    )
    expert_grads = (
        lax.psum_scatter(
            grad_first.astype(jnp.bfloat16), "dp", scatter_dimension=1, tiled=True
        ).astype(jnp.float32),
        lax.psum_scatter(
            grad_second.astype(jnp.bfloat16), "dp", scatter_dimension=2, tiled=True
        ).astype(jnp.float32),
    )
    probs_grad = jnp.sum(jnp.where(one_hot, gate_grad[:, :, None], 0.0), axis=1)
    logit_grad = (
        router_probs * (probs_grad - jnp.sum(router_probs * probs_grad, axis=-1, keepdims=True))
    ).astype(jnp.bfloat16)
    out_grad_b = out_grad.astype(jnp.bfloat16)
    shared_hidden_grad = matmul_nt(out_grad_b, shared_out_back)
    _, pull_shared = jax.vjp(swiglu, shared_join)
    shared_join_grad = pull_shared(shared_hidden_grad)[0].astype(jnp.bfloat16)
    grad_router = matmul_tn(normed_two_b, logit_grad)
    grad_shared_in = matmul_tn(normed_two_b, shared_join_grad)
    grad_shared_out = matmul_tn(shared_hidden_b, out_grad_b)
    normed_two_grad = (
        route_grad
        + matmul_nt(logit_grad, router_back)
        + matmul_nt(shared_join_grad, shared_in_back)
    )
    _, pull_norm_two = jax.vjp(rms_norm, middle, gain_two_back.astype(jnp.float32))
    middle_part, grad_gain_two = pull_norm_two(normed_two_grad)
    ffn_grads = (
        lax.psum_scatter(
            grad_gain_two.astype(jnp.bfloat16), "expert", scatter_dimension=0, tiled=True
        ).astype(jnp.float32),
        lax.psum_scatter(
            grad_router.astype(jnp.bfloat16), "expert", scatter_dimension=0, tiled=True
        ).astype(jnp.float32),
        lax.psum_scatter(
            grad_shared_in.astype(jnp.bfloat16), "expert", scatter_dimension=0, tiled=True
        ).astype(jnp.float32),
        lax.psum_scatter(
            grad_shared_out.astype(jnp.bfloat16), "expert", scatter_dimension=0, tiled=True
        ).astype(jnp.float32),
    )
    middle_grad = out_grad + middle_part
    middle_grad_b = middle_grad.astype(jnp.bfloat16)
    grad_out_w = matmul_tn(mixed_b, middle_grad_b)
    attn_grad_b = matmul_nt(middle_grad_b, out_back).reshape(row_count, H, DV).astype(jnp.bfloat16)
    row_delta = jnp.sum(attn_grad_b.astype(jnp.float32) * attn_full, axis=-1).T
    (query_nope_grad, query_rope_grad), key_terms = attend_grads(
        query_nope,
        query_rope,
        back_blocks,
        query_pos,
        prefix_end,
        score_scale,
        log_total,
        attn_grad_b,
        row_delta,
    )
    key_grad_all, value_grad_all, rope_grad_all = key_terms
    key_sums = (
        lax.psum_scatter(
            key_grad_all.reshape(-1, H * DN).astype(jnp.bfloat16),
            "expert",
            scatter_dimension=0,
            tiled=True,
        ).astype(jnp.float32),
        lax.psum_scatter(
            value_grad_all.reshape(-1, H * DV).astype(jnp.bfloat16),
            "expert",
            scatter_dimension=0,
            tiled=True,
        ).astype(jnp.float32),
        lax.psum_scatter(
            rope_grad_all.reshape(-1, DR).astype(jnp.bfloat16),
            "expert",
            scatter_dimension=0,
            tiled=True,
        ).astype(jnp.float32),
    )
    nope_sum, value_sum, rope_sum = key_sums
    kv_up_grad = (
        jnp.concatenate(
            [nope_sum.reshape(row_count, H, DN), value_sum.reshape(row_count, H, DV)], axis=-1
        )
        .reshape(row_count, H * (DN + DV))
        .astype(jnp.bfloat16)
    )
    grad_kv_up = matmul_tn(latent_b, kv_up_grad)
    latent_upstream = matmul_nt(kv_up_grad, kv_up_back)
    _, pull_latent = jax.vjp(rms_norm, latent, kv_gain_back.astype(jnp.float32))
    latent_grad, grad_kv_gain = pull_latent(latent_upstream)
    _, pull_key_rope = jax.vjp(
        lambda rope_part: rotate(rope_part, cosine, sine_table), kv_down[:, KVR:]
    )
    kv_down_grad = jnp.concatenate([latent_grad, pull_key_rope(rope_sum)[0]], axis=1).astype(
        jnp.bfloat16
    )
    grad_kv_down = matmul_tn(normed_b, kv_down_grad)
    _, pull_query_rope = jax.vjp(
        lambda rope_part: rotate(rope_part, cosine[:, None, :], sine_table[:, None, :]),
        query_raw[..., DN:],
    )
    query_grad = (
        jnp.concatenate([query_nope_grad, pull_query_rope(query_rope_grad)[0]], axis=-1)
        .reshape(row_count, H * (DN + DR))
        .astype(jnp.bfloat16)
    )
    grad_query = matmul_tn(normed_b, query_grad)
    normed_grad = matmul_nt(query_grad, query_back) + matmul_nt(kv_down_grad, kv_down_back)
    _, pull_norm_one = jax.vjp(rms_norm, values, gain_one_back.astype(jnp.float32))
    input_part, grad_gain_one = pull_norm_one(normed_grad)
    grad_tokens = middle_grad + input_part
    attn_grads = (
        lax.psum_scatter(
            grad_gain_one.astype(jnp.bfloat16), "expert", scatter_dimension=0, tiled=True
        ).astype(jnp.float32),
        lax.psum_scatter(
            grad_query.astype(jnp.bfloat16), "expert", scatter_dimension=0, tiled=True
        ).astype(jnp.float32),
        lax.psum_scatter(
            grad_kv_down.astype(jnp.bfloat16), "expert", scatter_dimension=0, tiled=True
        ).astype(jnp.float32),
        lax.psum_scatter(
            grad_kv_gain.astype(jnp.bfloat16), "expert", scatter_dimension=0, tiled=True
        ).astype(jnp.float32),
        lax.psum_scatter(
            grad_kv_up.astype(jnp.bfloat16), "expert", scatter_dimension=0, tiled=True
        ).astype(jnp.float32),
        lax.psum_scatter(
            grad_out_w.astype(jnp.bfloat16), "expert", scatter_dimension=0, tiled=True
        ).astype(jnp.float32),
    )
    summed = (
        lax.psum(attn_grads[0].astype(jnp.bfloat16), "dp").astype(jnp.float32),
        lax.psum(attn_grads[1].astype(jnp.bfloat16), "dp").astype(jnp.float32),
        lax.psum(attn_grads[2].astype(jnp.bfloat16), "dp").astype(jnp.float32),
        lax.psum(attn_grads[3].astype(jnp.bfloat16), "dp").astype(jnp.float32),
        lax.psum(attn_grads[4].astype(jnp.bfloat16), "dp").astype(jnp.float32),
        lax.psum(attn_grads[5].astype(jnp.bfloat16), "dp").astype(jnp.float32),
        lax.psum(ffn_grads[0].astype(jnp.bfloat16), "dp").astype(jnp.float32),
        lax.psum(ffn_grads[1].astype(jnp.bfloat16), "dp").astype(jnp.float32),
        lax.psum(ffn_grads[2].astype(jnp.bfloat16), "dp").astype(jnp.float32),
        lax.psum(ffn_grads[3].astype(jnp.bfloat16), "dp").astype(jnp.float32),
    )
    return (
        out,
        grad_tokens,
        summed[0],
        summed[1],
        summed[2],
        summed[3],
        summed[4],
        summed[5],
        summed[6],
        summed[7],
        summed[8],
        summed[9],
        expert_grads[0],
        expert_grads[1],
    )


def solution(mesh):
    placed = (
        P(("dp", "expert"), None),
        P(("dp", "expert"), None),
        P("dp"),
        P(("dp", "expert"), None),
        P("expert"),
        P("expert", None),
        P("expert", None),
        P("expert"),
        P("expert", None),
        P("expert", None),
        P("expert"),
        P("expert", None),
        P("expert", None),
        P("expert", None),
        P("expert", "dp", None),
        P("expert", None, "dp"),
    )
    return jax.shard_map(
        body,
        mesh=mesh,
        in_specs=placed,
        out_specs=(
            P(("dp", "expert"), None),
            P(("dp", "expert"), None),
            P("expert"),
            P("expert", None),
            P("expert", None),
            P("expert"),
            P("expert", None),
            P("expert", None),
            P("expert"),
            P("expert", None),
            P("expert", None),
            P("expert", None),
            P("expert", "dp", None),
            P("expert", None, "dp"),
        ),
        check_vma=False,
    )
```

profile of v0, /device:TPU:0, one launch (start us, length us, event | category | flops | bytes accessed | tf_op | source)
XLA Modules:
  0.0 2688.7 jit_solution(2181333764619170589)
XLA Ops:
  48.2 44.6 %all-gather.15.cloned.1.call-done = bf16[512,4096]{1,0:T(8,128)(2,1)} async-done(((bf16[64,4096]{1,0:T(8,128)(2,1)}), bf16[512,4096]{1,0:T(8,128)(2,1)}) %all-gather.15.cloned.1.call-update) | async-done | bytes 4194320 | tf_op jit(solution)/shard_map/all_gather | solution.py:287
  162.9 28.8 %all-gather.21.cloned.1.call-done = bf16[1024,2048]{1,0:T(8,128)(2,1)} async-done(((bf16[128,2048]{1,0:T(8,128)(2,1)}), bf16[1024,2048]{1,0:T(8,128)(2,1)}) %all-gather.21.cloned.1.call-update) | async-done | bytes 4194320 | tf_op jit(solution)/shard_map/all_gather | solution.py:323
  198.3 110.3 %all-gather.19.cloned.1.call-done = bf16[2048,3072]{1,0:T(8,128)(2,1)} async-done(((bf16[256,3072]{1,0:T(8,128)(2,1)}), bf16[2048,3072]{1,0:T(8,128)(2,1)}) %all-gather.19.cloned.1.call-update) | async-done | bytes 12582928 | tf_op jit(solution)/shard_map/all_gather | solution.py:284
  334.8 22.5 while.44
  358.1 32.3 %all-gather.23.cloned.1.call-done = bf16[2048,2048]{1,0:T(8,128)(2,1)} async-done(((bf16[256,2048]{1,0:T(8,128)(2,1)}), bf16[2048,2048]{1,0:T(8,128)(2,1)}) %all-gather.23.cloned.1.call-update) | async-done | bytes 8388624 | tf_op jit(solution)/shard_map/all_gather | solution.py:288
  449.1 80.0 %all-to-all-done.2 = bf16[2,8,72,2048]{3,2,0,1:T(8,128)(2,1)} async-done(((bf16[2,8,72,2048]{3,2,0,1:T(8,128)(2,1)}), bf16[2,8,72,2048]{3,2,0,1:T(8,128)(2,1)}, u32[]{:S(2)}, u32[]{:S(2)}) %all-to-all-start.2) | async-done | bytes 4718624 | tf_op jit(solution)/shard_map/all_to_all | solution.py:419
  539.6 99.5 %all-to-all-done = bf16[2,8,72,2048]{3,2,0,1:T(8,128)(2,1)} async-done(((bf16[2,8,72,2048]{3,2,0,1:T(8,128)(2,1)}), bf16[2,8,72,2048]{3,2,0,1:T(8,128)(2,1)}, u32[]{:S(2)}, u32[]{:S(2)}) %all-to-all-start) | async-done | bytes 4718624 | tf_op jit(solution)/shard_map/all_to_all | solution.py:353
  644.3 23.4 fusion.144
  667.7 48.6 %all-gather.31.cloned.1.call-done = bf16[2,1408,2048]{2,1,0:T(8,128)(2,1)} async-done(((bf16[2,1408,512]{2,1,0:T(8,128)(2,1)}), bf16[2,1408,2048]{2,1,0:T(8,128)(2,1)}) %all-gather.31.cloned.1.call-update) | async-done | bytes 11534352 | tf_op jit(solution)/shard_map/all_gather | solution.py:363
  780.9 206.4 %all-to-all-done.1 = bf16[2,8,72,2048]{3,2,0,1:T(8,128)(2,1)} async-done(((bf16[2,8,72,2048]{3,2,0,1:T(8,128)(2,1)}), bf16[2,8,72,2048]{3,2,0,1:T(8,128)(2,1)}, u32[]{:S(2)}, u32[]{:S(2)}) %all-to-all-start.1) | async-done | bytes 4718624 | tf_op jit(solution)/shard_map/all_to_all | solution.py:371
  993.2 101.9 %all-gather.25.cloned.1.call-done = bf16[2048,5632]{1,0:T(8,128)(2,1)} async-done(((bf16[256,5632]{1,0:T(8,128)(2,1)}), bf16[2048,5632]{1,0:T(8,128)(2,1)}) %all-gather.25.cloned.1.call-update) | async-done | bytes 23068688 | tf_op jit(solution)/shard_map/all_gather | solution.py:291
  1108.0 107.4 %all-gather.27.cloned.1.call-done = bf16[2816,2048]{1,0:T(8,128)(2,1)} async-done(((bf16[352,2048]{1,0:T(8,128)(2,1)}), bf16[2816,2048]{1,0:T(8,128)(2,1)}) %all-gather.27.cloned.1.call-update) | async-done | bytes 11534352 | tf_op jit(solution)/shard_map/all_gather | solution.py:292
  1308.5 31.4 %while.45 = (s32[]{:T(128)}, f32[128,16,128]{2,0,1:T(8,128)}, f32[128,16,64]{0,2,1:T(8,128)}, bf16[2,512,16,128]{3,1,2,0:T(8,128)(2,1)}, bf16[2,512,16,128]{3,1,...) while((s32[]{:T(128)}, f32[128,16,128]{2,0,1:T(8,128)}, ...), condition=%wide.region_31.32_spmd, body=%wide.region_28.31_spmd.sunk | while | flops 1756300800 | bytes 103767168 | solution.py:237
  1360.1 23.1 reduce-scatter.37.cloned.1.call-done
  1384.2 50.0 %reduce-scatter.15.cloned.1.call-done = bf16[128,2048]{1,0:T(8,128)(2,1)} async-done(((bf16[1024,2048]{1,0:T(8,128)(2,1)}), bf16[128,2048]{1,0:T(8,128)(2,1)}) %reduce-scatter.15.cloned.1.call-update) | async-done | bytes 524304 | tf_op jit(solution)/shard_map/reduce_scatter | solution.py:502
  1435.4 50.0 %reduce-scatter.17.cloned.1.call-done = bf16[128,2048]{1,0:T(8,128)(2,1)} async-done(((bf16[1024,2048]{1,0:T(8,128)(2,1)}), bf16[128,2048]{1,0:T(8,128)(2,1)}) %reduce-scatter.17.cloned.1.call-update) | async-done | bytes 524304 | tf_op jit(solution)/shard_map/reduce_scatter | solution.py:508
  1550.9 26.5 convolution_convert_fusion.1
  1578.1 90.0 %reduce-scatter.25.cloned.1.call-done = bf16[256,2048]{1,0:T(8,128)(2,1)} async-done(((bf16[2048,2048]{1,0:T(8,128)(2,1)}), bf16[256,2048]{1,0:T(8,128)(2,1)}) %reduce-scatter.25.cloned.1.call-update) | async-done | bytes 1048592 | tf_op jit(solution)/shard_map/reduce_scatter | solution.py:570
  1668.2 120.5 %reduce-scatter.31.cloned.1.call-done = bf16[352,2048]{1,0:T(8,128)(2,1)} async-done(((bf16[2816,2048]{1,0:T(8,128)(2,1)}), bf16[352,2048]{1,0:T(8,128)(2,1)}) %reduce-scatter.31.cloned.1.call-update) | async-done | bytes 1441808 | tf_op jit(solution)/shard_map/reduce_scatter | solution.py:480
  1788.7 129.9 %reduce-scatter.19.cloned.1.call-done = bf16[256,3072]{1,0:T(8,128)(2,1)} async-done(((bf16[2048,3072]{1,0:T(8,128)(2,1)}), bf16[256,3072]{1,0:T(8,128)(2,1)}) %reduce-scatter.19.cloned.1.call-update) | async-done | bytes 1572880 | tf_op jit(solution)/shard_map/reduce_scatter | solution.py:558
  1918.6 228.3 %reduce-scatter.29.cloned.1.call-done = bf16[256,5632]{1,0:T(8,128)(2,1)} async-done(((bf16[2048,5632]{1,0:T(8,128)(2,1)}), bf16[256,5632]{1,0:T(8,128)(2,1)}) %reduce-scatter.29.cloned.1.call-update) | async-done | bytes 2883600 | tf_op jit(solution)/shard_map/reduce_scatter | solution.py:477
  2193.8 97.7 %reduce-scatter.35.cloned.1.call-done = bf16[2,1408,512]{2,1,0:T(8,128)(2,1)} async-done(((bf16[2,1408,2048]{2,1,0:T(8,128)(2,1)}), bf16[2,1408,512]{2,1,0:T(8,128)(2,1)}) %reduce-scatter.35.cloned.1.call-update) | async-done | bytes 2883600 | tf_op jit(solution)/shard_map/reduce_scatter | solution.py:448
  2296.7 202.8 %reduce-scatter.33.cloned.1.call-done = bf16[2,512,2816]{2,1,0:T(8,128)(2,1)} async-done(((bf16[2,2048,2816]{2,1,0:T(8,128)(2,1)}), bf16[2,512,2816]{2,1,0:T(8,128)(2,1)}) %reduce-scatter.33.cloned.1.call-update) | async-done | bytes 5767184 | tf_op jit(solution)/shard_map/reduce_scatter | solution.py:445
  2507.4 161.9 %all-reduce.17.cloned.1.call-done = (bf16[256,3072]{1,0:T(8,128)(2,1)}, bf16[256,576]{0,1:T(8,128)(2,1)}, bf16[64,4096]{1,0:T(8,128)(2,1)}, bf16[256,2048]{1,0:T...) async-done(((bf16[256,3072]{1,0:T(8,128)(2,1)}, bf16[256,576]{0,1:T(8,128)(2,1)}, bf16[64,4096]{1,0:T(8,128)(2,1)}, bf16[256,2048]{1,0:T(8,128)(2,1)}, ...) | async-done | bytes 7766032 | tf_op jit(solution)/shard_map/psum | solution.py:576
  (458 shorter events, 641.2 us)
Async XLA Ops:
  8.7 147.6 %all-gather.17.cloned.1.call-start = ((), (), s32[]{:S(2)}) async-start(), calls=%async_computation.18 | async-start | bytes 4718592 | tf_op jit(solution)/shard_map/all_gather | solution.py:322
  97.3 94.5 %all-gather.21.cloned.1.call-start = ((), (), s32[]{:S(2)}) async-start(), calls=%async_computation.20 | async-start | bytes 4718592 | tf_op jit(solution)/shard_map/all_gather | solution.py:323
  98.3 210.4 %all-gather.19.cloned.1.call-start = ((), (), s32[]{:S(2)}) async-start(), calls=%async_computation.19 | async-start | bytes 14155776 | tf_op jit(solution)/shard_map/all_gather | solution.py:284
  98.9 291.6 %all-gather.23.cloned.1.call-start = ((), (), s32[]{:S(2)}) async-start(), calls=%async_computation.21 | async-start | bytes 9437184 | tf_op jit(solution)/shard_map/all_gather | solution.py:288
  99.4 544.9 %all-gather.29.cloned.1.call-start = ((), (), s32[]{:S(2)}) async-start(), calls=%async_computation.24 | async-start | bytes 28835840 | tf_op jit(solution)/shard_map/all_gather | solution.py:362
  100.2 616.0 %all-gather.31.cloned.1.call-start = ((), (), s32[]{:S(2)}) async-start(), calls=%async_computation.25 | async-start | bytes 14417920 | tf_op jit(solution)/shard_map/all_gather | solution.py:363
  101.0 994.2 %all-gather.25.cloned.1.call-start = ((), (), s32[]{:S(2)}) async-start(), calls=%async_computation.22 | async-start | bytes 25952256 | tf_op jit(solution)/shard_map/all_gather | solution.py:291
  419.3 109.8 %all-to-all-start.2 = ((bf16[2,8,72,2048]{3,2,0,1:T(8,128)(2,1)}), bf16[2,8,72,2048]{3,2,0,1:T(8,128)(2,1)}, u32[]{:S(2)}, u32[]{:S(2)}) async-start(bf16[2,8,72,2048]{3,2,0,1:T(8,128)(2,1)} %copy.218), calls=%async_computation.2 | async-start | bytes 9437184 | tf_op jit(solution)/shard_map/all_to_all | solution.py:419
  529.2 109.9 %all-to-all-start = ((bf16[2,8,72,2048]{3,2,0,1:T(8,128)(2,1)}), bf16[2,8,72,2048]{3,2,0,1:T(8,128)(2,1)}, u32[]{:S(2)}, u32[]{:S(2)}) async-start(bf16[2,8,72,2048]{3,2,0,1:T(8,128)(2,1)} %copy.213), calls=%async_computation | async-start | bytes 9437184 | tf_op jit(solution)/shard_map/all_to_all | solution.py:353
  533.8 681.6 %all-gather.27.cloned.1.call-start = ((), (), s32[]{:S(2)}) async-start(), calls=%async_computation.23 | async-start | bytes 12976128 | tf_op jit(solution)/shard_map/all_gather | solution.py:292
  748.7 238.6 %all-to-all-start.1 = ((bf16[2,8,72,2048]{3,2,0,1:T(8,128)(2,1)}), bf16[2,8,72,2048]{3,2,0,1:T(8,128)(2,1)}, u32[]{:S(2)}, u32[]{:S(2)}) async-start(bf16[2,8,72,2048]{3,2,0,1:T(8,128)(2,1)} %copy.215), calls=%async_computation.1 | async-start | bytes 9437184 | tf_op jit(solution)/shard_map/all_to_all | solution.py:371
  987.3 278.2 %all-to-all-start.3 = ((bf16[2,8,72,2048]{3,2,0,1:T(8,128)(2,1)}), bf16[2,8,72,2048]{3,2,0,1:T(8,128)(2,1)}, u32[]{:S(2)}, u32[]{:S(2)}) async-start(bf16[2,8,72,2048]{3,2,0,1:T(8,128)(2,1)} %copy.220), calls=%async_computation.3 | async-start | bytes 9437184 | tf_op jit(solution)/shard_map/all_to_all | solution.py:434
  992.0 391.2 %reduce-scatter.37.cloned.1.call-start = ((), (), s32[]{:S(2)}) async-start(), calls=%async_computation.37 | async-start | bytes 294912
  1341.7 92.6 %reduce-scatter.15.cloned.1.call-start = ((), (), s32[]{:S(2)}) async-start(), calls=%async_computation.26 | async-start | bytes 4718592 | tf_op jit(solution)/shard_map/reduce_scatter | solution.py:502
  1350.8 134.6 %reduce-scatter.17.cloned.1.call-start = ((), (), s32[]{:S(2)}) async-start(), calls=%async_computation.27 | async-start | bytes 4718592 | tf_op jit(solution)/shard_map/reduce_scatter | solution.py:508
  1360.1 217.5 %reduce-scatter.21.cloned.1.call-start = ((), (), s32[]{:S(2)}) async-start(), calls=%async_computation.29 | async-start | bytes 2654208 | tf_op jit(solution)/shard_map/reduce_scatter | solution.py:561
  1496.3 171.8 %reduce-scatter.25.cloned.1.call-start = ((), (), s32[]{:S(2)}) async-start(), calls=%async_computation.31 | async-start | bytes 9437184 | tf_op jit(solution)/shard_map/reduce_scatter | solution.py:570
  1502.0 286.7 %reduce-scatter.31.cloned.1.call-start = ((), (), s32[]{:S(2)}) async-start(), calls=%async_computation.34 | async-start | bytes 12976128 | tf_op jit(solution)/shard_map/reduce_scatter | solution.py:480
  1509.5 409.1 %reduce-scatter.19.cloned.1.call-start = ((), (), s32[]{:S(2)}) async-start(), calls=%async_computation.28 | async-start | bytes 14155776 | tf_op jit(solution)/shard_map/reduce_scatter | solution.py:558
  1520.4 626.5 %reduce-scatter.29.cloned.1.call-start = ((), (), s32[]{:S(2)}) async-start(), calls=%async_computation.33 | async-start | bytes 25952256 | tf_op jit(solution)/shard_map/reduce_scatter | solution.py:477
  1534.4 645.2 %reduce-scatter.27.cloned.1.call-start = ((), (), s32[]{:S(2)}) async-start(), calls=%async_computation.32 | async-start | bytes 73728 | tf_op jit(solution)/shard_map/reduce_scatter | solution.py:474
  1535.9 755.7 %reduce-scatter.35.cloned.1.call-start = ((), (), s32[]{:S(2)}) async-start(), calls=%async_computation.36 | async-start | bytes 14417920 | tf_op jit(solution)/shard_map/reduce_scatter | solution.py:448
  1550.5 949.0 %reduce-scatter.33.cloned.1.call-start = ((), (), s32[]{:S(2)}) async-start(), calls=%async_computation.35 | async-start | bytes 28835840 | tf_op jit(solution)/shard_map/reduce_scatter | solution.py:445
  1577.5 1091.9 %all-reduce.17.cloned.1.call-start = ((), (), s32[]{:S(2)}) async-start(), calls=%async_computation.38 | async-start | bytes 15532032 | tf_op jit(solution)/shard_map/psum | solution.py:576
  (100 other events, 4226.1 us)
Sparse Core Ops, SparseCore 0:
  9.6 35.7 all-gather.12
  47.0 45.7 all-gather.14
  97.4 46.3 all-gather.16
  145.8 45.9 all-gather.20
  193.2 115.4 all-gather.18
  310.1 80.2 all-gather.22
  392.3 208.4 all-gather.28
  602.6 113.6 all-gather.30
  717.9 377.1 all-gather.24
  1096.6 118.7 all-gather.26
  1341.8 41.3 reduce-scatter.36
  1386.0 48.1 reduce-scatter.14
  1437.2 48.1 reduce-scatter.16
  1491.7 34.4 reduce-scatter.20
  1529.0 49.0 reduce-scatter.22
  1580.4 87.7 reduce-scatter.24
  1671.0 117.6 reduce-scatter.30
  1791.0 127.5 reduce-scatter.18
  1921.0 225.8 reduce-scatter.28
  2149.6 28.4 reduce-scatter.26
  2181.2 110.3 reduce-scatter.34
  2294.7 204.7 reduce-scatter.32
  2504.7 164.6 all-reduce.16
where the time goes:
time: 2700 us; the launch traced here: 2690 us
  waiting for transfers between devices  2020 us (75%)
  matrix products  258 us (10%)
  local copies, waits for them, and re-layouts  185 us (7%)
  blocking collectives  90.2 us (3%)
  other arithmetic  76.6 us (3%)
    reduce_scatter x1, waiting for transfers between devices, body(): lax.psum_scatter(grad_shared_in.astype(jnp.bfloat16), 'expert', scatter_d...  228 us
    all_to_all x1, waiting for transfers between devices, body(): lax.all_to_all(result_b.reshape(owned, groups, capacity, D), 'expert', sp...  206 us
    reduce_scatter x1, waiting for transfers between devices, body(): lax.psum_scatter(grad_first.astype(jnp.bfloat16), 'dp', scatter_dimension...  203 us
    psum x1, waiting for transfers between devices, body(): lax.psum(attn_grads[1].astype(jnp.bfloat16), 'dp').astype(jnp.float32)  162 us
    reduce_scatter x1, waiting for transfers between devices, body(): lax.psum_scatter(grad_query.astype(jnp.bfloat16), 'expert', scatter_dimen...  130 us
    reduce_scatter x1, waiting for transfers between devices, body(): lax.psum_scatter(grad_shared_out.astype(jnp.bfloat16), 'expert', scatter_...  121 us
    all_gather x1, waiting for transfers between devices, body(): lax.all_gather(w_query, 'expert', axis=0, tiled=True)  110 us
    all_gather x1, waiting for transfers between devices, body(): lax.all_gather(shared_out, 'expert', axis=0, tiled=True)  107 us
  transfers between devices with their start and end apart: 27, of which 22 were waited for; matrix products, arithmetic and copies ran while one was open for 16% of the time, Pallas kernels for 0%

commit v1 on v0

--- a/solution.py
+++ b/solution.py
@@ -1,6 +1,11 @@
+import functools
+
 import jax
 import jax.numpy as jnp
 from jax import lax
+from jax.experimental import pallas as pl
+from jax.experimental.pallas import tpu as pltpu
+from jax.sharding import Mesh
 from jax.sharding import PartitionSpec as P
 
 D = 2048
@@ -601,44 +606,844 @@
     )
 
 
+def visible_scores(query, key, first_row, prefix_end, scale):
+    scores = scale * lax.dot_general(
+        query, key, (((1,), (1,)), ((), ())), preferred_element_type=jnp.float32
+    )
+    row = first_row + lax.broadcasted_iota(jnp.int32, scores.shape, 0)
+    column = lax.broadcasted_iota(jnp.int32, scores.shape, 1)
+    return jnp.where((column <= row) | (column < prefix_end), scores, MASKED)
+
+
+def head_operands(heads, head, query, key_rope, kv_up):
+    at = head * (DN + DV)
+    rope = heads * DN + head * DR
+    query_h = jnp.concatenate(
+        [query[:, head * DN : (head + 1) * DN], query[:, rope : rope + DR]], axis=1
+    )
+    key_h = jnp.concatenate([kv_up[:, at : at + DN], key_rope], axis=1)
+    return query_h, key_h, kv_up[:, at + DN : at + DN + DV]
+
+
+def attend_kernel(heads, scale, prefix_ref, query_ref, key_rope_ref, kv_up_ref, mixed_ref):
+    tile = query_ref.shape[0]
+    first_row = pl.program_id(0) * tile
+    query, key_rope, kv_up = query_ref[...], key_rope_ref[...], kv_up_ref[...]
+    for head in range(heads):
+        query_h, key_h, value_h = head_operands(heads, head, query, key_rope, kv_up)
+        scores = visible_scores(query_h, key_h, first_row, prefix_ref[0], scale)
+        powers = jnp.exp(scores - jnp.max(scores, axis=1, keepdims=True))
+        probs = powers * (1.0 / jnp.sum(powers, axis=1, keepdims=True))
+        mixed_ref[:, head * DV : (head + 1) * DV] = jnp.dot(
+            probs.astype(jnp.bfloat16), value_h, preferred_element_type=jnp.float32
+        ).astype(jnp.bfloat16)
+
+
+def attend_back_kernel(
+    heads, scale, prefix_ref, query_ref, grad_ref, key_rope_ref, kv_up_ref,
+    query_nope_ref, query_rope_ref, kv_grad_ref, rope_grad_ref, key_total, value_total,
+):
+    step = pl.program_id(0)
+    tile = query_ref.shape[0]
+
+    @pl.when(step == 0)
+    def _():
+        key_total[...] = jnp.zeros_like(key_total)
+        value_total[...] = jnp.zeros_like(value_total)
+
+    query, key_rope, kv_up = query_ref[...], key_rope_ref[...], kv_up_ref[...]
+    tn = (((0,), (0,)), ((), ()))
+    for head in range(heads):
+        query_h, key_h, value_h = head_operands(heads, head, query, key_rope, kv_up)
+        grad_h = grad_ref[:, head * DV : (head + 1) * DV]
+        scores = visible_scores(query_h, key_h, step * tile, prefix_ref[0], scale)
+        powers = jnp.exp(scores - jnp.max(scores, axis=1, keepdims=True))
+        probs = powers * (1.0 / jnp.sum(powers, axis=1, keepdims=True))
+        prob_grad = lax.dot_general(
+            grad_h, value_h, (((1,), (1,)), ((), ())), preferred_element_type=jnp.float32
+        )
+        delta = jnp.sum(probs * prob_grad, axis=1, keepdims=True)
+        dscore = (probs * (prob_grad - delta)).astype(jnp.bfloat16)
+        query_grad = scale * jnp.dot(dscore, key_h, preferred_element_type=jnp.float32)
+        query_nope_ref[:, head * DN : (head + 1) * DN] = query_grad[:, :DN].astype(jnp.bfloat16)
+        query_rope_ref[:, head * DR : (head + 1) * DR] = query_grad[:, DN:]
+        key_total[head] += lax.dot_general(dscore, query_h, tn, preferred_element_type=jnp.float32)
+        value_total[head] += lax.dot_general(
+            probs.astype(jnp.bfloat16), grad_h, tn, preferred_element_type=jnp.float32
+        )
+
+    @pl.when(step == pl.num_programs(0) - 1)
+    def _():
+        rope = jnp.zeros(rope_grad_ref.shape, jnp.float32)
+        for head in range(heads):
+            at = head * (DN + DV)
+            total = scale * key_total[head]
+            kv_grad_ref[:, at : at + DN] = total[:, :DN].astype(jnp.bfloat16)
+            kv_grad_ref[:, at + DN : at + DN + DV] = value_total[head].astype(jnp.bfloat16)
+            rope += total[:, DN:]
+        rope_grad_ref[...] = rope
+
+
+def attend(prefix, query, key_rope, kv_up, heads, scale):
+    length = query.shape[0]
+    tile = min(256, length)
+    whole = lambda value: pl.BlockSpec(value.shape, lambda i: (0, 0))
+    rows = lambda width: pl.BlockSpec((tile, width), lambda i: (i, 0))
+    return pl.pallas_call(
+        functools.partial(attend_kernel, heads, scale),
+        grid=(length // tile,),
+        out_shape=jax.ShapeDtypeStruct((length, heads * DV), jnp.bfloat16),
+        in_specs=[pl.BlockSpec(memory_space=pltpu.SMEM), rows(query.shape[1]), whole(key_rope), whole(kv_up)],
+        out_specs=rows(heads * DV),
+        compiler_params=pltpu.CompilerParams(vmem_limit_bytes=48 * 1024 * 1024),
+        cost_estimate=pl.CostEstimate(
+            flops=2 * heads * length * length * (DN + DR + DV),
+            transcendentals=heads * length * length,
+            bytes_accessed=2 * length * heads * (DN + DR + DN + DV + DV),
+        ),
+        name="attend",
+    )(prefix, query, key_rope, kv_up)
+
+
+def attend_back(prefix, query, grad, key_rope, kv_up, heads, scale):
+    length = query.shape[0]
+    tile = min(256, length)
+    whole = lambda shape: pl.BlockSpec(shape, lambda i: (0, 0))
+    rows = lambda width: pl.BlockSpec((tile, width), lambda i: (i, 0))
+    return pl.pallas_call(
+        functools.partial(attend_back_kernel, heads, scale),
+        grid=(length // tile,),
+        out_shape=[
+            jax.ShapeDtypeStruct((length, heads * DN), jnp.bfloat16),
+            jax.ShapeDtypeStruct((length, heads * DR), jnp.float32),
+            jax.ShapeDtypeStruct(kv_up.shape, jnp.bfloat16),
+            jax.ShapeDtypeStruct(key_rope.shape, jnp.float32),
+        ],
+        in_specs=[
+            pl.BlockSpec(memory_space=pltpu.SMEM),
+            rows(query.shape[1]),
+            rows(grad.shape[1]),
+            whole(key_rope.shape),
+            whole(kv_up.shape),
+        ],
+        out_specs=[rows(heads * DN), rows(heads * DR), whole(kv_up.shape), whole(key_rope.shape)],
+        scratch_shapes=[
+            pltpu.VMEM((heads, length, DN + DR), jnp.float32),
+            pltpu.VMEM((heads, length, DV), jnp.float32),
+        ],
+        compiler_params=pltpu.CompilerParams(vmem_limit_bytes=48 * 1024 * 1024),
+        cost_estimate=pl.CostEstimate(
+            flops=2 * heads * length * length * 3 * (DN + DR + DV),
+            transcendentals=heads * length * length,
+            bytes_accessed=2 * length * heads * 3 * (DN + DR + DN + DV + DV),
+        ),
+        name="attend_back",
+    )(prefix, query, grad, key_rope, kv_up)
+
+
+def expert_kernel(expert_count, spot, *refs):
+    x_in, g_in = refs[0:4], refs[4:8]
+    first_in, second_in, router = refs[8:10], refs[10:12], refs[12]
+    back_out = refs[13:17]
+    hidden_out, grads_out, rows_out, grad_rows_out, second_out, logit_out = refs[17:23]
+    first_w, second_w, x_buf, g_buf, back_st, hidden_st, grads_st, in_sem, w_sem, out_sem, keep_sem = refs[23:]
+    lane, core, expert = spot[0], spot[1], spot[2]
+    lanes = len(x_in)
+    rows = x_buf.shape[1]
+    depth, half = first_w.shape[1], first_w.shape[2]
+    slab = depth // lanes
+    side = half // 2
+
+    loads = []
+    for step in range(lanes):
+        loads.append(
+            (
+                pltpu.make_async_copy(x_in[step], x_buf.at[step], in_sem.at[0, step]),
+                pltpu.make_async_copy(g_in[step], g_buf.at[step], in_sem.at[1, step]),
+            )
+        )
+    first_loads, second_loads = [], []
+    for part in range(2):
+        slot = core if part == 0 else 1 - core
+        for step in range(lanes):
+            at = pl.multiple_of((lane ^ step) * slab, slab)
+            first_loads.append(
+                pltpu.make_async_copy(
+                    first_in[part].at[pl.ds(step * slab, slab), :], first_w.at[slot, pl.ds(at, slab), :], w_sem.at[0, part, step]
+                )
+            )
+            second_loads.append(
+                pltpu.make_async_copy(
+                    second_in[part].at[pl.ds(step * side, side), :],
+                    second_w.at[pl.ds(pl.multiple_of(slot * side, side), side), pl.ds(at, slab)],
+                    w_sem.at[1, part, step],
+                )
+            )
+    loads[0][0].start()
+    for copy in first_loads:
+        copy.start()
+    loads[0][1].start()
+    for copy in second_loads:
+        copy.start()
+    for step in range(1, lanes):
+        loads[step][0].start()
+        loads[step][1].start()
+
+    def kept(step):
+        where = pl.ds(step * rows, rows)
+        return [
+            pltpu.make_async_copy(x_buf.at[step], rows_out.at[where, :], keep_sem.at[step]),
+            pltpu.make_async_copy(g_buf.at[step], grad_rows_out.at[where, :], keep_sem.at[lanes + step]),
+        ]
+
+    second_kept = pltpu.make_async_copy(second_w, second_out, keep_sem.at[2 * lanes])
+
+    def stores(step, slot, back):
+        where = pl.ds(pl.multiple_of(step * rows, rows), rows)
+        return [
+            pltpu.make_async_copy(back_st.at[slot], back, out_sem.at[slot, 0]),
+            pltpu.make_async_copy(hidden_st.at[slot], hidden_out.at[where, :], out_sem.at[slot, 1]),
+            pltpu.make_async_copy(grads_st.at[slot, 0], grads_out.at[0, where, :], out_sem.at[slot, 2]),
+            pltpu.make_async_copy(grads_st.at[slot, 1], grads_out.at[1, where, :], out_sem.at[slot, 3]),
+        ]
+
+    nt = (((1,), (1,)), ((), ()))
+
+    def compute(step, slot):
+        x = x_buf[step]
+        a = jnp.dot(x, first_w[0], preferred_element_type=jnp.float32)
+        b = jnp.dot(x, first_w[1], preferred_element_type=jnp.float32)
+        logits = jnp.dot(x, router[...], preferred_element_type=jnp.float32)
+        column = lax.broadcasted_iota(jnp.int32, logits.shape, 1)
+        logits = jnp.where(column < expert_count, logits, -1e30)
+        top = jnp.max(logits, axis=1, keepdims=True)
+        powers = jnp.exp(logits - top)
+        probs = powers / jnp.sum(powers, axis=1, keepdims=True)
+        hot = (column == expert).astype(jnp.float32)
+        gate = jnp.sum(probs * hot, axis=1, keepdims=True)
+        g = g_buf[step]
+        up = lax.dot_general(g, second_w[...], nt, preferred_element_type=jnp.float32)
+        sig = 1.0 / (1.0 + jnp.exp(-a))
+        act = a * sig
+        hidden = act * b
+        hidden_st[slot] = (gate * hidden).astype(jnp.bfloat16)
+        gate_grad = jnp.sum(up * hidden, axis=1, keepdims=True)
+        up = up * gate
+        grad_b = (up * act).astype(jnp.bfloat16)
+        grad_a = (up * b * (sig + act * (1.0 - sig))).astype(jnp.bfloat16)
+        grads_st[slot, core] = grad_a
+        grads_st[slot, 1 - core] = grad_b
+        logit = (gate * gate_grad * (hot - probs)).astype(jnp.bfloat16)
+        logit_out[pl.ds(pl.multiple_of(step * rows, rows), rows), :] = logit
+        back = lax.dot_general(grad_a, first_w[0], nt, preferred_element_type=jnp.float32)
+        back += lax.dot_general(grad_b, first_w[1], nt, preferred_element_type=jnp.float32)
+        back += lax.dot_general(logit, router[...], nt, preferred_element_type=jnp.float32)
+        back_st[slot] = back.astype(jnp.bfloat16)
+
+    for copy in first_loads + second_loads:
+        copy.wait()
+    second_kept.start()
+
+    def body_step(step, carry):
+        slot = lax.rem(step, 2)
+        for i in range(lanes):
+
+            @pl.when(step == i)
+            def _():
+                loads[i][0].wait()
+                loads[i][1].wait()
+                for copy in kept(i):
+                    copy.start()
+
+        for i in range(2, lanes):
+
+            @pl.when(step == i)
+            def _():
+                for copy in stores(i - 2, i % 2, back_out[i - 2]):
+                    copy.wait()
+
+        compute(step, slot)
+        for i in range(lanes):
+
+            @pl.when(step == i)
+            def _():
+                for copy in stores(i, i % 2, back_out[i]):
+                    copy.start()
+
+        return carry
+
+    lax.fori_loop(0, lanes, body_step, 0)
+    for step in range(lanes - 2, lanes):
+        for copy in stores(step, step % 2, back_out[step]):
+            copy.wait()
+    for step in range(lanes):
+        for copy in kept(step):
+            copy.wait()
+    second_kept.wait()
+
+
+def expert_step(spot, x_pieces, g_pieces, first_mine, first_other, second_mine, second_other, router_wide, expert_count):
+    rows, depth = x_pieces[0].shape
+    half = first_mine.shape[1]
+    lanes = len(x_pieces)
+    total = rows * lanes
+    bf = jnp.bfloat16
+    any_spec = pl.BlockSpec(memory_space=pl.ANY)
+    vmem_spec = pl.BlockSpec(memory_space=pltpu.VMEM)
+    return pl.pallas_call(
+        functools.partial(expert_kernel, expert_count),
+        out_shape=[jax.ShapeDtypeStruct((rows, depth), bf)] * lanes
+        + [
+            jax.ShapeDtypeStruct((total, half), bf),
+            jax.ShapeDtypeStruct((2, total, half), bf),
+            jax.ShapeDtypeStruct((total, depth), bf),
+            jax.ShapeDtypeStruct((total, depth), bf),
+            jax.ShapeDtypeStruct((half, depth), bf),
+            jax.ShapeDtypeStruct((total, 128), bf),
+        ],
+        in_specs=[pl.BlockSpec(memory_space=pltpu.SMEM)] + [any_spec] * (2 * lanes + 4) + [vmem_spec],
+        out_specs=[any_spec] * (lanes + 5) + [vmem_spec],
+        scratch_shapes=[
+            pltpu.VMEM((2, depth, half), bf),
+            pltpu.VMEM((half, depth), bf),
+            pltpu.VMEM((lanes, rows, depth), bf),
+            pltpu.VMEM((lanes, rows, depth), bf),
+            pltpu.VMEM((2, rows, depth), bf),
+            pltpu.VMEM((2, rows, half), bf),
+            pltpu.VMEM((2, 2, rows, half), bf),
+            pltpu.SemaphoreType.DMA((2, lanes)),
+            pltpu.SemaphoreType.DMA((2, 2, lanes)),
+            pltpu.SemaphoreType.DMA((2, 4)),
+            pltpu.SemaphoreType.DMA((2 * lanes + 1,)),
+        ],
+        compiler_params=pltpu.CompilerParams(vmem_limit_bytes=60 * 1024 * 1024),
+        cost_estimate=pl.CostEstimate(
+            flops=10 * total * depth * half,
+            transcendentals=total * half,
+            bytes_accessed=2 * (3 * depth * half * 2 + total * (5 * depth + 3 * half)),
+        ),
+        name="expert_rows",
+    )(spot, *x_pieces, *g_pieces, first_mine, first_other, second_mine, second_other, router_wide)
+
+
+def shared_body(
+    tokens,
+    cotangent,
+    prefix,
+    routes,
+    norm1_gain,
+    w_query,
+    w_kv_down,
+    kv_gain,
+    w_kv_up,
+    w_out,
+    norm2_gain,
+    w_router,
+    shared_in,
+    shared_out,
+    expert_in,
+    expert_out,
+):
+    rows = tokens.shape[0]
+    topk = routes.shape[1]
+    chips = lax.axis_size("z")
+    lanes = lax.axis_size("dp")
+    groups = chips * 2
+    owned = expert_in.shape[0]
+    expert_count = owned * groups
+    capacity = 3 * rows * topk // (2 * expert_count)
+    heads = H // groups
+    length = rows * groups
+    scale = float(DN + DR) ** (-0.5)
+    my_dp = lax.axis_index("dp")
+    my_z = lax.axis_index("z")
+    my_core = lax.axis_index("core")
+    my_expert = my_z * 2 * owned + my_dp
+    group = ("z", "core")
+    hidden_n = shared_out.shape[0]
+    kv_cols = w_kv_down.shape[1]
+    half = expert_in.shape[2] // 2
+
+    def gather(value):
+        return lax.all_gather(value, group, axis=0, tiled=True)
+
+    def scatter_sum(value):
+        return lax.psum_scatter(value, group, scatter_dimension=0, tiled=True)
+
+    def fence(*values):
+        return lax.optimization_barrier(values)
+
+    def swap(value):
+        return lax.ppermute(value, "core", [(0, 1), (1, 0)])
+
+    def ordered(mine, other, axis):
+        return jnp.where(
+            my_core == 0,
+            jnp.concatenate([mine, other], axis=axis),
+            jnp.concatenate([other, mine], axis=axis),
+        )
+
+    def halves(value, axis):
+        size = value.shape[axis] // 2
+        mine = lax.dynamic_slice_in_dim(value, my_core * size, size, axis)
+        other = lax.dynamic_slice_in_dim(value, (1 - my_core) * size, size, axis)
+        return mine, other
+
+    def exchange(value):
+        return lax.all_to_all(value, group, split_axis=0, concat_axis=0, tiled=True)
+
+    def to_lane(value, step):
+        return lax.ppermute(value, "dp", [(lane, lane ^ step) for lane in range(lanes)])
+
+    def by_lane(pieces):
+        full = jnp.zeros((lanes,) + pieces[0].shape, pieces[0].dtype)
+        for step in range(lanes):
+            full = lax.dynamic_update_index_in_dim(full, pieces[step], my_dp ^ step, 0)
+        return full
+
+    def to_lanes(pieces):
+        return [pieces[0]] + [to_lane(pieces[step], step) for step in range(1, lanes)]
+
+    def lane_exchange(value):
+        return to_lanes(
+            [lax.dynamic_index_in_dim(value, my_dp ^ step, 0, keepdims=False) for step in range(lanes)]
+        )
+
+    def own_part(value):
+        part = value.shape[0] // lanes
+        return lax.dynamic_slice_in_dim(value, my_dp * part, part, 0).transpose(1, 0, 2)
+
+    share = norm1_gain.shape[0]
+    kv_share = kv_gain.shape[0]
+    used = kv_cols + expert_count
+    extra = 640 - used
+    gains = jnp.concatenate([norm1_gain, norm2_gain, kv_gain])
+    gain_rows = gains.shape[0] // extra
+    small = jnp.concatenate(
+        [
+            w_kv_down,
+            w_router,
+            jnp.concatenate(
+                [
+                    jnp.pad(gains.reshape(gain_rows, extra), ((0, share - rows - gain_rows), (0, 0))),
+                    jnp.pad(routes.astype(jnp.bfloat16), ((0, 0), (0, extra - topk))),
+                ]
+            ),
+        ],
+        axis=1,
+    )
+    query_n = heads * (DN + DR)
+    kv_width = heads * (DN + DV)
+    fold = share // kv_share
+    query_parts = w_query.reshape(share, groups, heads, DN + DR)
+    attention_parts = jnp.concatenate(
+        [
+            query_parts[..., :DN].reshape(share, groups, heads * DN),
+            query_parts[..., DN:].reshape(share, groups, heads * DR),
+            w_kv_up.reshape(kv_share, groups, fold, kv_width // fold)
+            .transpose(0, 2, 1, 3)
+            .reshape(share, groups, kv_width // fold),
+        ],
+        axis=2,
+    )
+    shared_parts = own_part(
+        shared_in.reshape(share, 2, groups, hidden_n)
+        .transpose(0, 2, 1, 3)
+        .reshape(share, groups, 2 * hidden_n)
+    )
+    tokens_all = gather(tokens)
+    small_all = gather(small)
+    attention_moved = exchange(own_part(attention_parts))
+    attention_pieces = to_lanes([attention_moved] * lanes)
+    def lane_pieces(value, axis):
+        keep, give = halves(value, axis)
+        received = swap(give)
+        pieces = []
+        for step in range(lanes):
+            lane = my_dp ^ step
+            pieces.append(
+                jnp.where(
+                    lane // 2 == my_core,
+                    lax.dynamic_index_in_dim(keep, lane % 2, 0, keepdims=False),
+                    lax.dynamic_index_in_dim(received, lane % 2, 0, keepdims=False),
+                )
+            )
+        return pieces
+
+    first_pieces = to_lanes(lane_pieces(expert_in, 2))
+    second_sources = lane_pieces(expert_out, 1)
+
+    shared_moved = exchange(shared_parts)
+    tokens_all, small_all, attention_pieces, first_pieces[:2], second_sources, shared_moved = fence(
+        tokens_all, small_all, attention_pieces, first_pieces[:2], second_sources, shared_moved
+    )
+    grad_all = gather(cotangent)
+    second_pieces = to_lanes(second_sources)
+    spare = small_all[:, used:].reshape(chips, 2, share, extra)
+    routes_mine = lax.dynamic_index_in_dim(
+        spare[:, :, share - rows :, :topk], my_core, axis=1, keepdims=False
+    ).astype(jnp.int32)
+
+    router_w = small_all[:, kv_cols:used]
+    gains_all = (
+        spare.reshape(groups, share, extra)[:, :gain_rows].reshape(groups, gain_rows * extra)
+    ).astype(jnp.float32)
+    gain_one = gains_all[:, :share].reshape(-1)
+    gain_two = gains_all[:, share : 2 * share].reshape(-1)
+    gain_kv = gains_all[:, 2 * share :].reshape(-1)
+    kv_down_w = small_all[:, :kv_cols]
+    attention_w = by_lane(attention_pieces).transpose(1, 0, 2, 3)
+    query_w = attention_w[..., :query_n].reshape(share * groups, query_n)
+    kv_up_w = attention_w[..., query_n:].reshape(kv_share * groups, kv_width)
+
+    plane = my_z * 2 * owned + (my_dp ^ jnp.arange(lanes, dtype=jnp.int32))
+    member = jnp.any(routes_mine[:, :, :, None] == plane[None, None, None, :], axis=2)
+    earlier = (jnp.arange(rows)[:, None] > jnp.arange(rows)[None, :]).astype(jnp.float32)
+    place = jnp.einsum(
+        "st,ztq->zqs", earlier, member.astype(jnp.float32), precision=lax.Precision.HIGHEST
+    )
+    slots = jnp.arange(capacity, dtype=jnp.float32)
+    pick = (
+        (place[:, :, None, :] == slots[None, None, :, None]) & member.transpose(0, 2, 1)[:, :, None, :]
+    ).astype(jnp.bfloat16)
+
+    def picked(blocks):
+        return [
+            jnp.einsum(
+                "zst,ztd->zsd", pick[:, step], blocks, preferred_element_type=jnp.float32
+            ).astype(jnp.bfloat16)
+            for step in range(lanes)
+        ]
+
+    def split_rows(value):
+        pieces = value.reshape(lanes, chips, capacity, D)
+        return [pieces[step] for step in range(lanes)]
+
+    def placed(pieces):
+        return jnp.einsum(
+            "zlst,zlsd->ztd", pick, jnp.stack(pieces, axis=1), preferred_element_type=jnp.float32
+        )
+
+    def my_blocks(value):
+        return lax.dynamic_index_in_dim(
+            value.reshape(chips, 2, rows, D), my_core, axis=1, keepdims=False
+        )
+
+    def add_mine(total, mine):
+        spread = jnp.where((jnp.arange(2) == my_core)[None, :, None, None], mine[:, None], 0.0)
+        return total.reshape(chips, 2, rows, D) + spread
+
+    positions = jnp.arange(length, dtype=jnp.int32)
+    cosine, sine_table = tables(positions, DR // 2)
+    values_all = tokens_all.astype(jnp.float32)
+    inverse_one = lax.rsqrt(jnp.mean(values_all * values_all, axis=-1, keepdims=True) + EPSILON)
+    normed_b = (values_all * inverse_one * gain_one).astype(jnp.bfloat16)
+    query_raw = matmul(normed_b, query_w)
+    query_rope = rotate(
+        query_raw[:, heads * DN :].reshape(length, heads, DR), cosine[:, None, :], sine_table[:, None, :]
+    )
+    query = jnp.concatenate(
+        [query_raw[:, : heads * DN], query_rope.reshape(length, heads * DR)], axis=1
+    ).astype(jnp.bfloat16)
+    kv_down = matmul(normed_b, kv_down_w)
+    latent = kv_down[:, :KVR]
+    inverse_kv = lax.rsqrt(jnp.mean(latent * latent, axis=-1, keepdims=True) + EPSILON)
+    latent_n = latent * inverse_kv
+    latent_b = (latent_n * gain_kv).astype(jnp.bfloat16)
+    key_rope = rotate(kv_down[:, KVR:], cosine, sine_table).astype(jnp.bfloat16)
+    kv_up = matmul(latent_b, kv_up_w).astype(jnp.bfloat16)
+    mixed_b = attend(prefix, query, key_rope, kv_up, heads, scale)
+    mixed_b, second_pieces, first_pieces = fence(mixed_b, second_pieces, first_pieces)
+    grad_picked = picked(my_blocks(grad_all))
+    attn_sum = scatter_sum(matmul(mixed_b, w_out).astype(jnp.bfloat16))
+    grad_pieces = to_lanes(grad_picked)
+    first_mine = jnp.concatenate(first_pieces)
+    first_other = swap(first_mine)
+
+    attn_sum, first_other, grad_pieces = fence(attn_sum, first_other, grad_pieces)
+    shared_pieces = to_lanes([shared_moved] * lanes)
+    second_mine = jnp.concatenate(second_pieces)
+    second_other = swap(second_mine)
+    middle = tokens.astype(jnp.float32) + attn_sum.astype(jnp.float32)
+
+    inverse_two = lax.rsqrt(jnp.mean(middle * middle, axis=-1, keepdims=True) + EPSILON)
+    normed_two_b = (middle * inverse_two * gain_two).astype(jnp.bfloat16)
+    x2 = gather(normed_two_b)
+    x2, shared_pieces, second_other = fence(x2, shared_pieces, second_other)
+    x_pieces = to_lanes(picked(my_blocks(x2)))
+    shared_w = by_lane(shared_pieces).transpose(1, 0, 2, 3).reshape(share * groups, 2 * hidden_n)
+
+    shared_a = matmul(x2, shared_w[:, :hidden_n])
+    shared_b = matmul(x2, shared_w[:, hidden_n:])
+    shared_sig = jax.nn.sigmoid(shared_a)
+    shared_hidden = (shared_a * shared_sig * shared_b).astype(jnp.bfloat16)
+    shared_part = matmul(shared_hidden, shared_out).astype(jnp.bfloat16)
+    shared_up = matmul_nt(grad_all, shared_out)
+    shared_ga = (shared_up * shared_b * shared_sig * (1.0 + shared_a * (1.0 - shared_sig))).astype(
+        jnp.bfloat16
+    )
+    shared_gb = (shared_up * shared_a * shared_sig).astype(jnp.bfloat16)
+    shared_g = jnp.concatenate([shared_ga, shared_gb], axis=1)
+    grad_shared_out = matmul_tn(shared_hidden, grad_all).astype(jnp.bfloat16)
+    grad_shared_in = matmul_tn(x2, shared_g).astype(jnp.bfloat16)
+    shared_back = matmul_nt(shared_g, shared_w).astype(jnp.bfloat16)
+    x_pieces, shared_part, shared_back, grad_shared_out, grad_shared_in = fence(
+        x_pieces, shared_part, shared_back, grad_shared_out, grad_shared_in
+    )
+
+    def lane_parts(value):
+        count = value.shape[0] // groups
+        return lane_exchange(
+            value.reshape(groups, lanes, count // lanes, value.shape[1]).transpose(1, 0, 2, 3)
+        )
+
+    def lane_rows(value):
+        return lane_exchange(value.reshape(lanes, value.shape[0] // lanes, value.shape[1]))
+
+    def lane_sum(pieces):
+        return sum(piece.astype(jnp.float32) for piece in pieces).astype(jnp.bfloat16)
+
+    flat = (chips * capacity, D)
+    part = share // lanes
+    shared_parts = lane_exchange(
+        jnp.concatenate(
+            [
+                grad_shared_in.reshape(groups, lanes, part, 2 * hidden_n)
+                .transpose(1, 0, 2, 3)
+                .reshape(lanes, groups * part, 2 * hidden_n),
+                grad_shared_out.reshape(lanes, -1, 2 * hidden_n),
+            ],
+            axis=1,
+        )
+    )
+    router_lane = kv_cols - KVR
+    spot = jnp.stack([my_dp, my_core, my_expert]).astype(jnp.int32)
+    step_out = expert_step(
+        spot,
+        [piece.reshape(flat) for piece in x_pieces],
+        [piece.reshape(flat) for piece in grad_pieces],
+        first_mine,
+        first_other,
+        second_mine,
+        second_other,
+        jnp.pad(router_w, ((0, 0), (0, 128 - expert_count))),
+        expert_count,
+    )
+    step_out, shared_parts = fence(step_out, shared_parts)
+    rows_grad = step_out[:lanes]
+    row_hidden, grads, x_rows, grad_rows, second_w, logit_grad = step_out[lanes:]
+    back_pieces = to_lanes([piece.reshape(chips, capacity, D) for piece in rows_grad])
+    grad_second = matmul_tn(row_hidden, grad_rows).astype(jnp.bfloat16)
+    result_b = matmul(row_hidden, second_w).astype(jnp.bfloat16)
+    logit_wide = jnp.pad(
+        logit_grad[:, :expert_count], ((0, 0), (router_lane, 128 - router_lane - expert_count))
+    )
+    grad_router = matmul_tn(x_rows, logit_wide)
+    shared_sum = lane_sum(shared_parts)
+    back_pieces, grad_second, grad_router, result_b, x_rows, grads, shared_sum = fence(
+        back_pieces, grad_second, grad_router, result_b, x_rows, grads, shared_sum
+    )
+    shared_in_moved = exchange(shared_sum[: groups * part].reshape(groups, part, 2 * hidden_n))
+    shared_out_own = shared_sum[groups * part :].reshape(part, -1)
+    grad_first_other = matmul_tn(x_rows, grads[1]).astype(jnp.bfloat16)
+    grad_first_mine = matmul_tn(x_rows, grads[0]).astype(jnp.bfloat16)
+
+    result_pieces = to_lanes(split_rows(result_b))
+    first_sent = swap(grad_first_other)
+    second_hold, second_send = halves(grad_second, 0)
+    second_sent = swap(second_send)
+    back_part = add_mine(shared_back.astype(jnp.float32), placed(back_pieces)).astype(jnp.bfloat16)
+    normed_two_grad = scatter_sum(back_part.reshape(length, D))
+    normed_two_grad, first_sent, second_sent, grad_first_mine = fence(
+        normed_two_grad, first_sent, second_sent, grad_first_mine
+    )
+    normed_two_grad = normed_two_grad.astype(jnp.float32)
+    normal_two = middle * inverse_two
+    grad_gain_two = jnp.sum(normed_two_grad * normal_two, axis=0)
+    scaled = normed_two_grad * gain_two
+    middle_grad = cotangent.astype(jnp.float32) + inverse_two * (
+        scaled - normal_two * jnp.mean(scaled * normal_two, axis=-1, keepdims=True)
+    )
+    grad_first = (grad_first_mine.astype(jnp.float32) + first_sent.astype(jnp.float32)).astype(jnp.bfloat16)
+    first_back = lane_exchange(grad_first.reshape(lanes, D // lanes, half))
+    grad_second = (second_hold.astype(jnp.float32) + second_sent.astype(jnp.float32)).astype(jnp.bfloat16)
+
+    middle_all = gather(middle_grad.astype(jnp.bfloat16))
+    middle_all, result_pieces, grad_second, shared_in_moved = fence(
+        middle_all, result_pieces, grad_second, shared_in_moved
+    )
+    early = jnp.concatenate(
+        [
+            shared_in_moved.reshape(groups, part, 2, hidden_n)
+            .transpose(1, 2, 0, 3)
+            .reshape(part, 2 * groups * hidden_n),
+            shared_out_own,
+        ],
+        axis=1,
+    )
+    early_pieces = to_lanes([early] * lanes)
+    out_part = add_mine(shared_part.astype(jnp.float32), placed(result_pieces)).astype(jnp.bfloat16)
+    ffn = scatter_sum(out_part.reshape(length, D))
+    second_back = lane_exchange(
+        grad_second.reshape(half // 2, lanes, D // lanes).transpose(1, 0, 2)
+    )
+    attn_grad = matmul_nt(middle_all, w_out).astype(jnp.bfloat16)
+    query_nope_grad, query_rope_grad, kv_up_grad, rope_grad = attend_back(
+        prefix, query, attn_grad, key_rope, kv_up, heads, scale
+    )
+    query_nope_grad, query_rope_grad, kv_up_grad, rope_grad, first_back, early_pieces = fence(
+        query_nope_grad, query_rope_grad, kv_up_grad, rope_grad, first_back, early_pieces
+    )
+    grad_out_w = matmul_tn(mixed_b, middle_all).astype(jnp.bfloat16)
+    out_w_parts = lane_rows(grad_out_w)
+
+    def own_slices(pieces, axis):
+        def of_core(core):
+            near = my_dp // 2 == core
+            pair = [jnp.where(near, pieces[i], pieces[2 + i]) for i in range(2)]
+            flip = my_dp % 2 == 1
+            return jnp.stack(
+                [jnp.where(flip, pair[1], pair[0]), jnp.where(flip, pair[0], pair[1])]
+            )
+
+        return ordered(of_core(my_core), swap(of_core(1 - my_core)), axis).astype(jnp.float32)
+
+    grad_kv_up = matmul_tn(latent_b, kv_up_grad).astype(jnp.bfloat16)
+    latent_up = matmul_nt(kv_up_grad, kv_up_w)
+    grad_kv_gain = jnp.sum(latent_up * latent_n, axis=0)
+    latent_scaled = latent_up * gain_kv
+    latent_grad = inverse_kv * (
+        latent_scaled - latent_n * jnp.mean(latent_scaled * latent_n, axis=-1, keepdims=True)
+    )
+    rope_grad = rotate(rope_grad, cosine, -sine_table)
+    kv_down_grad = jnp.concatenate([latent_grad, rope_grad], axis=1).astype(jnp.bfloat16)
+    query_rope_grad = rotate(
+        query_rope_grad.reshape(length, heads, DR), cosine[:, None, :], -sine_table[:, None, :]
+    )
+    query_grad = jnp.concatenate(
+        [query_nope_grad, query_rope_grad.reshape(length, heads * DR).astype(jnp.bfloat16)], axis=1
+    )
+    normed_part = matmul_nt(query_grad, query_w) + matmul_nt(kv_down_grad, kv_down_w)
+    grad_gain_one = jnp.sum(normed_part * (values_all * inverse_one), axis=0)
+    normed_part, ffn = fence(normed_part.astype(jnp.bfloat16), ffn)
+    grad_query = matmul_tn(normed_b, query_grad).astype(jnp.bfloat16)
+    attention_grad = jnp.concatenate(
+        [
+            grad_query.reshape(groups, share, query_n),
+            grad_kv_up.reshape(groups, share, kv_width // fold),
+        ],
+        axis=2,
+    ).reshape(groups * share, query_n + kv_width // fold)
+    attention_moved = exchange(lane_sum(lane_parts(attention_grad)))
+
+    kv_wide = jnp.pad(kv_down_grad, ((0, 0), (0, 640 - kv_cols)))
+    gains_grad = jnp.concatenate(
+        [
+            grad_gain_one.reshape(groups, share),
+            grad_gain_two.reshape(groups, share),
+            grad_kv_gain.reshape(groups, kv_share),
+        ],
+        axis=1,
+    ).reshape(groups, gain_rows, extra)
+    gains_wide = jnp.pad(
+        gains_grad, ((0, 0), (0, share - gain_rows), (128 - extra, 0))
+    ).reshape(groups * share, 128)
+    small_grad = (
+        matmul_tn(normed_b, kv_wide) + jnp.pad(grad_router + gains_wide, ((0, 0), (KVR, 0)))
+    ).astype(jnp.bfloat16)
+    small_sum = scatter_sum(small_grad)
+    small_sum, normed_part = fence(small_sum, normed_part)
+    normed_grad = scatter_sum(normed_part)
+    small_part = lane_sum(lane_rows(small_sum))
+
+    grad_first = own_slices(first_back, 2)
+    grad_second = own_slices(second_back, 1)
+    def lane_gather(value):
+        return lax.all_gather(value, "dp", axis=0, tiled=True)
+
+    early = by_lane(early_pieces).reshape(share, -1)
+    cut = 2 * groups * hidden_n
+    shared_in_grad = early[:, :cut].astype(jnp.float32)
+    shared_out_grad = early[:, cut:].reshape(hidden_n, D).astype(jnp.float32)
+    query_cols = attention_moved[..., :query_n].transpose(1, 0, 2)
+    query_cols = jnp.concatenate(
+        [
+            query_cols[..., : heads * DN].reshape(part, groups, heads, DN),
+            query_cols[..., heads * DN :].reshape(part, groups, heads, DR),
+        ],
+        axis=-1,
+    ).reshape(part, H * (DN + DR))
+    kv_cols_grad = (
+        attention_moved[..., query_n:]
+        .reshape(groups, part // fold, fold, kv_width // fold)
+        .transpose(1, 2, 0, 3)
+        .reshape(part, groups * kv_width // fold)
+    )
+    late = jnp.concatenate([query_cols, kv_cols_grad, lane_sum(out_w_parts), small_part], axis=1)
+    late, normed_grad = fence(late, normed_grad)
+    late = lane_gather(late)
+    cut = H * (DN + DR)
+    query_grad_out = late[:, :cut].astype(jnp.float32)
+    kv_up_grad_out = (
+        late[:, cut : cut + groups * kv_width // fold]
+        .reshape(kv_share, fold, groups, kv_width // fold)
+        .transpose(0, 2, 1, 3)
+        .reshape(kv_share, H * (DN + DV))
+        .astype(jnp.float32)
+    )
+    cut += groups * kv_width // fold
+    out_w_grad = late[:, cut : cut + D].astype(jnp.float32)
+    small_sum = late[:, cut + D :].astype(jnp.float32)
+    gains_sum = small_sum[:gain_rows, used:].reshape(-1)
+
+    out = (middle + ffn.astype(jnp.float32)).astype(jnp.bfloat16)
+    normed_grad = normed_grad.astype(jnp.float32)
+    values = tokens.astype(jnp.float32)
+    inverse_own = lax.rsqrt(jnp.mean(values * values, axis=-1, keepdims=True) + EPSILON)
+    normal_one = values * inverse_own
+    scaled_one = normed_grad * gain_one
+    grad_tokens = middle_grad + inverse_own * (
+        scaled_one - normal_one * jnp.mean(scaled_one * normal_one, axis=-1, keepdims=True)
+    )
+    return (
+        out,
+        grad_tokens,
+        gains_sum[:share],
+        query_grad_out,
+        small_sum[:, :kv_cols],
+        gains_sum[2 * share :],
+        kv_up_grad_out,
+        out_w_grad,
+        gains_sum[share : 2 * share],
+        small_sum[:, kv_cols:used],
+        shared_in_grad,
+        shared_out_grad,
+        grad_first,
+        grad_second,
+    )
+
+
 def solution(mesh):
-    placed = (
-        P(("dp", "expert"), None),
-        P(("dp", "expert"), None),
-        P("dp"),
-        P(("dp", "expert"), None),
-        P("expert"),
-        P("expert", None),
-        P("expert", None),
-        P("expert"),
-        P("expert", None),
-        P("expert", None),
-        P("expert"),
-        P("expert", None),
-        P("expert", None),
-        P("expert", None),
-        P("expert", "dp", None),
-        P("expert", None, "dp"),
-    )
+    groups = mesh.shape["expert"]
+    lanes = mesh.shape["dp"]
+    if H % groups == 0 and groups % 2 == 0 and lanes == 4:
+        inner = Mesh(mesh.devices.reshape(lanes, groups // 2, 2), ("dp", "z", "core"))
+        return sharded(shared_body, inner, "dp", ("z", "core"))
+    return sharded(body, mesh, "dp", "expert")
+
+
+def sharded(function, mesh, dp, expert):
+    every = (dp, expert) if isinstance(expert, str) else (dp,) + expert
+    row = P(every, None)
+    vector = P(expert)
+    matrix = P(expert, None)
+    first = P(expert, dp, None)
+    second = P(expert, None, dp)
+    weights = (vector, matrix, matrix, vector, matrix, matrix, vector, matrix, matrix, matrix, first, second)
     return jax.shard_map(
-        body,
+        function,
         mesh=mesh,
-        in_specs=placed,
-        out_specs=(
-            P(("dp", "expert"), None),
-            P(("dp", "expert"), None),
-            P("expert"),
-            P("expert", None),
-            P("expert", None),
-            P("expert"),
-            P("expert", None),
-            P("expert", None),
-            P("expert"),
-            P("expert", None),
-            P("expert", None),
-            P("expert", None),
-            P("expert", "dp", None),
-            P("expert", None, "dp"),
-        ),
+        in_specs=(row, row, P(dp), row) + weights,
+        out_specs=(row, row) + weights,
         check_vma=False,
     )

time: 2700 us -> 1040 us (0.39)
  waiting for transfers between devices: 2020 us -> 447 us
  matrix products: 258 us -> 137 us
  blocking collectives: 90.2 us -> 0 us
  Pallas kernels: 0 us -> 78.7 us
  starting transfers between devices: 20.8 us -> 78.4 us
  other arithmetic: 76.6 us -> 111 us
  local copies, waits for them, and re-layouts: 185 us -> 158 us
    reduce_scatter x11 -> x5, waiting for transfers between devices: 970 us -> 22 us  [scatter_sum(): return lax.psum_scatter(value, group, scatter_dimension=0, tiled=True)]
    all_gather x10 -> x6, waiting for transfers between devices: 478 us -> 32.9 us  [the longest x5 16.8 us: gather(): return lax.all_gather(value, group, axis=0, tiled=True)]
    ppermute x0 -> x53, waiting for transfers between devices: none -> 364 us  [the longest x45 364 us: to_lane(): lax.ppermute(value, 'dp', [(lane, lane ^ step) for lane in range(lanes)])]
    all_to_all x4, waiting for transfers between devices: 386 us -> 27.6 us  [exchange(): return lax.all_to_all(value, group, split_axis=0, concat_axis=0, tiled=True)]
    psum x1 -> x0, waiting for transfers between devices: 162 us -> none  [body(): lax.psum(attn_grads[1].astype(jnp.bfloat16), 'dp').astype(jnp.float32)]
    dot_general x18 -> x11, matrix products: 136 us -> 18.2 us  [the longest x8 12.5 us: picked(): jnp.einsum('zst,ztd->zsd', pick[:, step], blocks, preferred_element_type=...]
    pallas_call x0 -> x3, Pallas kernels: none -> 78.7 us  [the longest x1 60.6 us: expert_step(): pl.pallas_call(functools.partial(expert_kernel, expert_count), out_shape=...]
    ppermute x0 -> x53, starting transfers between devices: none -> 58.6 us  [the longest x45 57.1 us: to_lane(): lax.ppermute(value, 'dp', [(lane, lane ^ step) for lane in range(lanes)])]
  transfers between devices with their start and end apart: 27 -> 68, of which waited for: 22 -> 32; matrix products, arithmetic and copies ran while one was open for 16% -> 31% of each run, Pallas kernels for 0% -> 8%
where the time goes in v1:
time: 1040 us; the launch traced here: 1030 us
  waiting for transfers between devices  447 us (43%)
  local copies, waits for them, and re-layouts  158 us (15%)
  matrix products  137 us (13%)
  other arithmetic  111 us (11%)
  Pallas kernels  78.7 us (8%)
  starting transfers between devices  78.4 us (8%)
  between operations  16.8 us (2%)
    ppermute x45, waiting for transfers between devices, to_lane(): lax.ppermute(value, 'dp', [(lane, lane ^ step) for lane in range(lanes)])  364 us
    dot_general x10, matrix products, matmul_tn(): lax.dot_general(left_side, right_side, (((0,), (0,)), ((), ())), preferre...  62.7 us
    pallas_call x1, Pallas kernels, expert_step(): pl.pallas_call(functools.partial(expert_kernel, expert_count), out_shape=...  60.6 us
    ppermute x45, starting transfers between devices, to_lane(): lax.ppermute(value, 'dp', [(lane, lane ^ step) for lane in range(lanes)])  57.1 us
    unnamed x198, local copies, waits for them, and re-layouts  46 us
    dot_general x8, matrix products, matmul(): return jnp.dot(left_side, right_side, preferred_element_type=jnp.float32)  28.9 us
    all_to_all x4, waiting for transfers between devices, exchange(): return lax.all_to_all(value, group, split_axis=0, concat_axis=0, tiled=True)  27.6 us
    dot_general x6, matrix products, matmul_nt(): lax.dot_general(left_side, right_side, (((1,), (1,)), ((), ())), preferre...  27.2 us
  transfers between devices with their start and end apart: 68, of which 32 were waited for; matrix products, arithmetic and copies ran while one was open for 31% of the time, Pallas kernels for 8%

profile of v1, /device:TPU:0, one launch (start us, length us, event | category | flops | bytes accessed | tf_op | source)
XLA Modules:
  0.0 1027.5 jit_solution(1288333840547584924)
XLA Ops:
  73.9 17.0 %collective-permute-done = bf16[8,64,512]{2,1,0:T(8,128)(2,1)} collective-permute-done((bf16[8,64,512]{2,1,0:T(8,128)(2,1)S(1)}, bf16[8,64,512]{2,1,0:T(8,128)(2,1)}, u32[]{:S(2)}, u32[]{:S(2)}) %collective-permute-start) | collective-permute-done | bytes 524320 | tf_op jit(solution)/shard_map/ppermute | solution.py:996
  103.3 15.3 %all-gather.7.cloned.1.call-done = bf16[1024,2048]{1,0:T(8,128)(2,1)} async-done(((bf16[128,2048]{1,0:T(8,128)(2,1)}), bf16[1024,2048]{1,0:T(8,128)(2,1)}) %all-gather.7.cloned.1.call-update) | async-done | bytes 4194320 | tf_op jit(solution)/shard_map/all_gather | solution.py:968
  164.5 30.2 %collective-permute-done.7 = bf16[704,512]{1,0:T(8,128)(2,1)} collective-permute-done((bf16[704,512]{1,0:T(8,128)(2,1)}, bf16[704,512]{1,0:T(8,128)(2,1)}, u32[]{:S(2)}, u32[]{:S(2)}) %collective-permute-start.7) | collective-permute-done | bytes 720928 | tf_op jit(solution)/shard_map/ppermute | solution.py:996
  218.8 23.8 %collective-permute-done.12 = bf16[4,72,2048]{2,1,0:T(8,128)(2,1)S(1)} collective-permute-done((bf16[4,72,2048]{2,1,0:T(8,128)(2,1)S(1)}, bf16[4,72,2048]{2,1,0:T(8,128)(2,1)S(1)}, u32[]{:S(2)}, u32[]{:S(2)}) %collective-permute-start.12) | collective-permute-done | bytes 1179680 | tf_op jit(solution)/shard_map/ppermute | solution.py:996
  242.6 26.2 %collective-permute-done.13 = bf16[4,72,2048]{2,1,0:T(8,128)(2,1)S(1)} collective-permute-done((bf16[4,72,2048]{2,1,0:T(8,128)(2,1)S(1)}, bf16[4,72,2048]{2,1,0:T(8,128)(2,1)S(1)}, u32[]{:S(2)}, u32[]{:S(2)}) %collective-permute-start.13) | collective-permute-done | bytes 1179680 | tf_op jit(solution)/shard_map/ppermute | solution.py:996
  303.3 16.6 %collective-permute-done.16 = bf16[8,64,704]{2,1,0:T(8,128)(2,1)} collective-permute-done((bf16[8,64,704]{2,1,0:T(8,128)(2,1)}, bf16[8,64,704]{2,1,0:T(8,128)(2,1)}, u32[]{:S(2)}, u32[]{:S(2)}) %collective-permute-start.16) | collective-permute-done | bytes 720928 | tf_op jit(solution)/shard_map/ppermute | solution.py:996
  357.5 14.1 %collective-permute-done.21 = bf16[4,72,2048]{2,1,0:T(8,128)(2,1)S(1)} collective-permute-done((bf16[4,72,2048]{2,1,0:T(8,128)(2,1)S(1)}, bf16[4,72,2048]{2,1,0:T(8,128)(2,1)S(1)}, u32[]{:S(2)}, u32[]{:S(2)}) %collective-permute-start.21) | collective-permute-done | bytes 1179680 | tf_op jit(solution)/shard_map/ppermute | solution.py:996
  371.6 24.5 %collective-permute-done.20 = bf16[4,72,2048]{2,1,0:T(8,128)(2,1)S(1)} collective-permute-done((bf16[4,72,2048]{2,1,0:T(8,128)(2,1)S(1)}, bf16[4,72,2048]{2,1,0:T(8,128)(2,1)S(1)}, u32[]{:S(2)}, u32[]{:S(2)}) %collective-permute-start.20) | collective-permute-done | bytes 1179680 | tf_op jit(solution)/shard_map/ppermute | solution.py:996
  423.3 60.6 %expert_rows.1 = (bf16[288,2048]{1,0:T(8,128)(2,1)}, bf16[288,2048]{1,0:T(8,128)(2,1)}, bf16[288,2048]{1,0:T(8,128)(2,1)}, bf16[288,2048]{1,0:T(8,128)(2,1)}, bf...) custom-call(s32[3]{0:T(128)} %pad_add_fusion.spot, ...), custom_call_target="tpu_custom_call" | custom-call | flops 33218887680 | bytes 67928064 | tf_op jit(solution)/shard_map/expert_rows/pallas_call | solution.py:893
  488.8 13.0 %convolution_convert_fusion.3 = bf16[1408,2048]{1,0:T(8,128)(2,1)} fusion(bf16[1152,1408]{1,0:T(8,128)(2,1)} %get-tuple-element.178, bf16[1152,2048]{1,0:T(8,128)(2,1)} %get-tuple-element.179), kind=kOutput, calls=%fused_computation.21 | convolution fusion | flops 6646661120 | bytes 13729792 | tf_op jit(solution)/shard_map/dot_general | solution.py:60
  516.8 22.3 %collective-permute-done.26 = bf16[4,72,2048]{2,1,0:T(8,128)(2,1)S(1)} collective-permute-done((bf16[4,72,2048]{2,1,0:T(8,128)(2,1)}, bf16[4,72,2048]{2,1,0:T(8,128)(2,1)S(1)}, u32[]{:S(2)}, u32[]{:S(2)}) %collective-permute-start.26) | collective-permute-done | bytes 1179680 | tf_op jit(solution)/shard_map/ppermute | solution.py:996
  544.2 11.4 %convolution_convert_fusion.1 = bf16[2048,1408]{1,0:T(8,128)(2,1)S(1)} fusion(bf16[1152,2048]{1,0:T(8,128)(2,1)} %get-tuple-element.192, bf16[2,1152,1408]{2,1,0:T(8,128)(2,1)} %get-tuple-element.193), kind=kOutput, calls=%fused_computation.19 | convolution fusion | flops 6646661120 | bytes 13729792 | tf_op jit(solution)/shard_map/dot_general | solution.py:60
  558.3 12.8 %convolution_convert_fusion = bf16[2048,1408]{1,0:T(8,128)(2,1)} fusion(bf16[1152,2048]{1,0:T(8,128)(2,1)} %get-tuple-element.192, bf16[2,1152,1408]{2,1,0:T(8,128)(2,1)} %get-tuple-element.193), kind=kOutput, calls=%fused_computation.18 | convolution fusion | flops 6646661120 | bytes 13729792 | tf_op jit(solution)/shard_map/dot_general | solution.py:60
  571.1 22.0 %reduce-scatter.8.cloned.1.call-done = bf16[128,2048]{1,0:T(8,128)(2,1)} async-done(((bf16[1024,2048]{1,0:T(8,128)(2,1)}), bf16[128,2048]{1,0:T(8,128)(2,1)}) %reduce-scatter.8.cloned.1.call-update) | async-done | bytes 524304 | tf_op jit(solution)/shard_map/reduce_scatter | solution.py:971
  617.9 19.6 %collective-permute-done.30 = bf16[4,72,2048]{2,1,0:T(8,128)(2,1)S(1)} collective-permute-done((bf16[4,72,2048]{2,1,0:T(8,128)(2,1)S(1)}, bf16[4,72,2048]{2,1,0:T(8,128)(2,1)S(1)}, u32[]{:S(2)}, u32[]{:S(2)}) %collective-permute-start.30) | collective-permute-done | bytes 1179680 | tf_op jit(solution)/shard_map/ppermute | solution.py:996
  637.5 24.3 %collective-permute-done.31 = bf16[4,72,2048]{2,1,0:T(8,128)(2,1)S(1)} collective-permute-done((bf16[4,72,2048]{2,1,0:T(8,128)(2,1)S(1)}, bf16[4,72,2048]{2,1,0:T(8,128)(2,1)S(1)}, u32[]{:S(2)}, u32[]{:S(2)}) %collective-permute-start.31) | collective-permute-done | bytes 1179680 | tf_op jit(solution)/shard_map/ppermute | solution.py:996
  690.8 22.5 %collective-permute-done.33 = bf16[512,1408]{1,0:T(8,128)(2,1)} collective-permute-done((bf16[512,1408]{1,0:T(8,128)(2,1)}, bf16[512,1408]{1,0:T(8,128)(2,1)}, u32[]{:S(2)}, u32[]{:S(2)}) %collective-permute-start.33) | collective-permute-done | bytes 1441824 | tf_op jit(solution)/shard_map/ppermute | solution.py:996
  720.0 11.7 %attend_back.1 = (bf16[1024,256]{1,0:T(8,128)(2,1)S(1)}, f32[1024,128]{1,0:T(8,128)S(1)}, bf16[1024,512]{1,0:T(8,128)(2,1)S(1)}, f32[1024,64]{1,0:T(8,128)S(1)}) custom-call(s32[1]{0:T(128)S(6)} %copy.423.prefix_ref, bf16[1024,384]{1,0:T(8,128)(2,1)S(1)} %pad_maximum_fusion.7.query_ref, bf16[1024,256]{1,0:T(8,128)(2,1)S(1)} %convolution_convert_fusion.21.grad_ref, ...), custom_call_target="tpu_custom_call" | custom-call | flops 4026531840 | bytes 7077888 | tf_op jit(solution)/shard_map/attend_back/pallas_call | solution.py:713
  731.7 15.1 %collective-permute-done.34 = bf16[512,1408]{1,0:T(8,128)(2,1)} collective-permute-done((bf16[512,1408]{1,0:T(8,128)(2,1)}, bf16[512,1408]{1,0:T(8,128)(2,1)}, u32[]{:S(2)}, u32[]{:S(2)}) %collective-permute-start.34) | collective-permute-done | bytes 1441824 | tf_op jit(solution)/shard_map/ppermute | solution.py:996
  746.7 20.7 %collective-permute-done.36 = bf16[64,8448]{1,0:T(8,128)(2,1)} collective-permute-done((bf16[64,8448]{1,0:T(8,128)(2,1)}, bf16[64,8448]{1,0:T(8,128)(2,1)}, u32[]{:S(2)}, u32[]{:S(2)}) %collective-permute-start.36) | collective-permute-done | bytes 1081376 | tf_op jit(solution)/shard_map/ppermute | solution.py:996
  767.4 23.9 %collective-permute-done.37 = bf16[64,8448]{1,0:T(8,128)(2,1)} collective-permute-done((bf16[64,8448]{1,0:T(8,128)(2,1)}, bf16[64,8448]{1,0:T(8,128)(2,1)}, u32[]{:S(2)}, u32[]{:S(2)}) %collective-permute-start.37) | collective-permute-done | bytes 1081376 | tf_op jit(solution)/shard_map/ppermute | solution.py:996
  859.9 13.7 %collective-permute-done.50 = bf16[704,512]{1,0:T(8,128)(2,1)} collective-permute-done((bf16[704,512]{1,0:T(8,128)(2,1)}, bf16[704,512]{1,0:T(8,128)(2,1)}, u32[]{:S(2)}, u32[]{:S(2)}) %collective-permute-start.50) | collective-permute-done | bytes 720928 | tf_op jit(solution)/shard_map/ppermute | solution.py:996
  932.7 20.2 %all-to-all-done.3 = bf16[8,64,512]{2,1,0:T(8,128)(2,1)S(1)} async-done(((bf16[8,64,512]{2,1,0:T(8,128)(2,1)}), bf16[8,64,512]{2,1,0:T(8,128)(2,1)S(1)}, u32[]{:S(2)}, u32[]{:S(2)}) %all-to-all-start.3) | async-done | bytes 524320 | tf_op jit(solution)/shard_map/all_to_all | solution.py:993
  990.9 16.1 %all-gather.17.cloned.1.call-done = bf16[256,6784]{1,0:T(8,128)(2,1)} async-done(((bf16[64,6784]{1,0:T(8,128)(2,1)}), bf16[256,6784]{1,0:T(8,128)(2,1)}) %all-gather.17.cloned.1.call-update) | async-done | bytes 3473424 | tf_op jit(solution)/shard_map/all_gather | solution.py:1362
  (533 shorter events, 513.1 us)
Async XLA Ops:
  7.2 96.1 %all-gather.9.cloned.1.call-start = ((), (), s32[]{:S(2)}) async-start(), calls=%async_computation.10 | async-start | bytes 2949120 | tf_op jit(solution)/shard_map/all_gather | solution.py:968
  11.8 106.8 %all-gather.7.cloned.1.call-start = ((), (), s32[]{:S(2)}) async-start(), calls=%async_computation.9 | async-start | bytes 4718592 | tf_op jit(solution)/shard_map/all_gather | solution.py:968
  30.4 178.5 %all-gather.11.cloned.1.call-start = ((), (), s32[]{:S(2)}) async-start(), calls=%async_computation.12 | async-start | bytes 4718592 | tf_op jit(solution)/shard_map/all_gather | solution.py:968
  62.2 208.8 %reduce-scatter.6.cloned.1.call-start = ((), (), s32[]{:S(2)}) async-start(), calls=%async_computation.11 | async-start | bytes 4718592 | tf_op jit(solution)/shard_map/reduce_scatter | solution.py:971
  71.5 89.3 %collective-permute-start.10 = (bf16[512,1408]{1,0:T(8,128)(2,1)}, bf16[512,1408]{1,0:T(8,128)(2,1)}, u32[]{:S(2)}, u32[]{:S(2)}) collective-permute-start(bf16[512,1408]{1,0:T(8,128)(2,1)} %get-tuple-element.339), channel_id=1, source_target_pairs={{0,24},{8,16},{16,8},{24,0},{1,25},{9,17},{17,9},{25,1},{2,26},{10... | collective-permute-start | bytes 4325384 | tf_op jit(solution)/shard_map/ppermute | solution.py:996
  91.0 73.5 %collective-permute-start.9 = (bf16[512,1408]{1,0:T(8,128)(2,1)}, bf16[512,1408]{1,0:T(8,128)(2,1)}, u32[]{:S(2)}, u32[]{:S(2)}) collective-permute-start(bf16[512,1408]{1,0:T(8,128)(2,1)} %get-tuple-element.340), channel_id=1, source_target_pairs={{0,16},{8,24},{16,0},{24,8},{1,17},{9,25},{17,1},{25,9},{2,18},{10... | collective-permute-start | bytes 4325384 | tf_op jit(solution)/shard_map/ppermute | solution.py:996
  198.0 123.4 %all-gather.13.cloned.1.call-start = ((), (), s32[]{:S(2)}) async-start(), calls=%async_computation.13 | async-start | bytes 4718592 | tf_op jit(solution)/shard_map/all_gather | solution.py:968
  274.3 318.8 %reduce-scatter.8.cloned.1.call-start = ((), (), s32[]{:S(2)}) async-start(), calls=%async_computation.14 | async-start | bytes 4718592 | tf_op jit(solution)/shard_map/reduce_scatter | solution.py:971
  415.1 70.1 %collective-permute-start.22 = (bf16[768,704]{0,1:T(8,128)(2,1)}, bf16[768,704]{0,1:T(8,128)(2,1)}, u32[]{:S(2)}, u32[]{:S(2)}) collective-permute-start(bf16[768,704]{0,1:T(8,128)(2,1)} %bitcast.364), channel_id=1, source_target_pairs={{0,8},{8,0},{16,24},{24,16},{1,9},{9,1},{17,25},{25,17},{2,10},{10... | collective-permute-start | bytes 3244040 | tf_op jit(solution)/shard_map/ppermute | solution.py:996
  418.9 66.3 %collective-permute-start.23 = (bf16[768,704]{0,1:T(8,128)(2,1)}, bf16[768,704]{0,1:T(8,128)(2,1)}, u32[]{:S(2)}, u32[]{:S(2)}) collective-permute-start(bf16[768,704]{0,1:T(8,128)(2,1)} %bitcast.365), channel_id=1, source_target_pairs={{0,16},{8,24},{16,0},{24,8},{1,17},{9,25},{17,1},{25,9},{2,18},{10... | collective-permute-start | bytes 3244040 | tf_op jit(solution)/shard_map/ppermute | solution.py:996
  422.1 63.1 %collective-permute-start.24 = (bf16[768,704]{0,1:T(8,128)(2,1)}, bf16[768,704]{0,1:T(8,128)(2,1)}, u32[]{:S(2)}, u32[]{:S(2)}) collective-permute-start(bf16[768,704]{0,1:T(8,128)(2,1)} %bitcast.366), channel_id=1, source_target_pairs={{0,24},{8,16},{16,8},{24,0},{1,25},{9,17},{17,9},{25,1},{2,26},{10... | collective-permute-start | bytes 3244040 | tf_op jit(solution)/shard_map/ppermute | solution.py:996
  544.1 119.5 %all-gather.15.cloned.1.call-start = ((), (), s32[]{:S(2)}) async-start(), calls=%async_computation.15 | async-start | bytes 4718592 | tf_op jit(solution)/shard_map/all_gather | solution.py:968
  599.8 63.8 %all-to-all-start.2 = ((bf16[8,64,704]{2,1,0:T(8,128)(2,1)}), bf16[8,64,704]{2,1,0:T(8,128)(2,1)S(1)}, u32[]{:S(2)}, u32[]{:S(2)}) async-start(bf16[8,64,704]{2,1,0:T(8,128)(2,1)} %bitcast.87), calls=%async_computation.4 | async-start | bytes 1572864 | tf_op jit(solution)/shard_map/all_to_all | solution.py:993
  604.0 291.3 %reduce-scatter.10.cloned.1.call-start = ((), (), s32[]{:S(2)}) async-start(), calls=%async_computation.16 | async-start | bytes 4718592 | tf_op jit(solution)/shard_map/reduce_scatter | solution.py:971
  670.0 225.3 %reduce-scatter.12.cloned.1.call-start = ((), (), s32[]{:S(2)}) async-start(), calls=%async_computation.17 | async-start | bytes 2949120 | tf_op jit(solution)/shard_map/reduce_scatter | solution.py:971
  680.6 66.2 %collective-permute-start.34 = (bf16[512,1408]{1,0:T(8,128)(2,1)}, bf16[512,1408]{1,0:T(8,128)(2,1)}, u32[]{:S(2)}, u32[]{:S(2)}) collective-permute-start(bf16[512,1408]{1,0:T(8,128)(2,1)} %get-tuple-element.350), channel_id=1, source_target_pairs={{0,16},{8,24},{16,0},{24,8},{1,17},{9,25},{17,1},{25,9},{2,18},{10... | collective-permute-start | bytes 4325384 | tf_op jit(solution)/shard_map/ppermute | solution.py:996
  683.0 63.7 %collective-permute-start.35 = (bf16[512,1408]{1,0:T(8,128)(2,1)}, bf16[512,1408]{1,0:T(8,128)(2,1)}, u32[]{:S(2)}, u32[]{:S(2)}) collective-permute-start(bf16[512,1408]{1,0:T(8,128)(2,1)} %get-tuple-element.349), channel_id=1, source_target_pairs={{0,24},{8,16},{16,8},{24,0},{1,25},{9,17},{17,9},{25,1},{2,26},{10... | collective-permute-start | bytes 4325384 | tf_op jit(solution)/shard_map/ppermute | solution.py:996
  687.6 79.8 %collective-permute-start.36 = (bf16[64,8448]{1,0:T(8,128)(2,1)}, bf16[64,8448]{1,0:T(8,128)(2,1)}, u32[]{:S(2)}, u32[]{:S(2)}) collective-permute-start(bf16[64,8448]{1,0:T(8,128)(2,1)} %constant_dynamic-update-slice_fusion.8), channel_id=1, source_target_pairs={{0,8},{8,0},{16,24},{24,16},{1,9},{9,1},{17,25},{25,17},{2,10},{10... | collective-permute-start | bytes 3244040 | tf_op jit(solution)/shard_map/ppermute | solution.py:996
  688.8 102.6 %collective-permute-start.37 = (bf16[64,8448]{1,0:T(8,128)(2,1)}, bf16[64,8448]{1,0:T(8,128)(2,1)}, u32[]{:S(2)}, u32[]{:S(2)}) collective-permute-start(bf16[64,8448]{1,0:T(8,128)(2,1)} %constant_dynamic-update-slice_fusion.8), channel_id=1, source_target_pairs={{0,16},{8,24},{16,0},{24,8},{1,17},{9,25},{17,1},{25,9},{2,18},{10... | collective-permute-start | bytes 3244040 | tf_op jit(solution)/shard_map/ppermute | solution.py:996
  713.3 78.1 %collective-permute-start.38 = (bf16[64,8448]{1,0:T(8,128)(2,1)}, bf16[64,8448]{1,0:T(8,128)(2,1)}, u32[]{:S(2)}, u32[]{:S(2)}) collective-permute-start(bf16[64,8448]{1,0:T(8,128)(2,1)} %constant_dynamic-update-slice_fusion.8), channel_id=1, source_target_pairs={{0,24},{8,16},{16,8},{24,0},{1,25},{9,17},{17,9},{25,1},{2,26},{10... | collective-permute-start | bytes 3244040 | tf_op jit(solution)/shard_map/ppermute | solution.py:996
  817.4 144.8 %reduce-scatter.14.cloned.1.call-start = ((), (), s32[]{:S(2)}) async-start(), calls=%async_computation.18 | async-start | bytes 4718592 | tf_op jit(solution)/shard_map/reduce_scatter | solution.py:971
  883.1 93.5 %collective-permute-start.52 = (bf16[2,704,512]{2,1,0:T(8,128)(2,1)}, bf16[2,704,512]{2,1,0:T(8,128)(2,1)}, u32[]{:S(2)}, u32[]{:S(2)}) collective-permute-start(bf16[2,704,512]{2,1,0:T(8,128)(2,1)} %pad_maximum_fusion.2), channel_id=1, source_target_pairs={{0,1},{1,0},{2,3},{3,2},{4,5},{5,4},{6,7},{7,6},{8,9},{9,8},{10,11... | collective-permute-start | bytes 4325384 | tf_op jit(solution)/shard_map/ppermute | solution.py:977
  890.2 90.8 %collective-permute-start.48 = (bf16[2,512,1408]{2,1,0:T(8,128)(2,1)}, bf16[2,512,1408]{2,1,0:T(8,128)(2,1)}, u32[]{:S(2)}, u32[]{:S(2)}) collective-permute-start(bf16[2,512,1408]{2,1,0:T(8,128)(2,1)} %pad_maximum_fusion), channel_id=1, source_target_pairs={{0,1},{1,0},{2,3},{3,2},{4,5},{5,4},{6,7},{7,6},{8,9},{9,8},{10,11... | collective-permute-start | bytes 8650760 | tf_op jit(solution)/shard_map/ppermute | solution.py:977
  930.4 76.6 %all-gather.17.cloned.1.call-start = ((), (), s32[]{:S(2)}) async-start(), calls=%async_computation.19 | async-start | bytes 4341760 | tf_op jit(solution)/shard_map/all_gather | solution.py:1362
  (134 other events, 3025.2 us)
Sparse Core Ops, SparseCore 0:
  11.9 47.8 all-gather.8
  61.4 57.1 all-gather.6
  120.2 46.0 all-gather.10
  198.1 51.1 reduce-scatter.5
  274.4 46.8 all-gather.12
  544.3 48.7 reduce-scatter.7
  597.6 62.8 all-gather.14
  670.1 51.2 reduce-scatter.9
  817.5 37.5 reduce-scatter.11
  895.5 55.8 reduce-scatter.13
  962.3 44.5 all-gather.16

commit v2 on v1

--- a/solution.py
+++ b/solution.py
@@ -733,7 +733,7 @@
         ],
         compiler_params=pltpu.CompilerParams(vmem_limit_bytes=48 * 1024 * 1024),
         cost_estimate=pl.CostEstimate(
-            flops=2 * heads * length * length * 3 * (DN + DR + DV),
+            flops=40 * heads * length * length * 3 * (DN + DR + DV),
             transcendentals=heads * length * length,
             bytes_accessed=2 * length * heads * 3 * (DN + DR + DN + DV + DV),
         ),
@@ -1073,10 +1073,10 @@
     first_pieces = to_lanes(lane_pieces(expert_in, 2))
     second_sources = lane_pieces(expert_out, 1)
 
+    tokens_all, small_all, attention_pieces, first_pieces[:2], second_sources, shared_parts = fence(
+        tokens_all, small_all, attention_pieces, first_pieces[:2], second_sources, shared_parts
+    )
     shared_moved = exchange(shared_parts)
-    tokens_all, small_all, attention_pieces, first_pieces[:2], second_sources, shared_moved = fence(
-        tokens_all, small_all, attention_pieces, first_pieces[:2], second_sources, shared_moved
-    )
     grad_all = gather(cotangent)
     second_pieces = to_lanes(second_sources)
     spare = small_all[:, used:].reshape(chips, 2, share, extra)
@@ -1152,15 +1152,16 @@
     latent_b = (latent_n * gain_kv).astype(jnp.bfloat16)
     key_rope = rotate(kv_down[:, KVR:], cosine, sine_table).astype(jnp.bfloat16)
     kv_up = matmul(latent_b, kv_up_w).astype(jnp.bfloat16)
+    query, kv_up, first_pieces = fence(query, kv_up, first_pieces)
     mixed_b = attend(prefix, query, key_rope, kv_up, heads, scale)
-    mixed_b, second_pieces, first_pieces = fence(mixed_b, second_pieces, first_pieces)
+    mixed_b, shared_moved, second_pieces = fence(mixed_b, shared_moved, second_pieces)
     grad_picked = picked(my_blocks(grad_all))
     attn_sum = scatter_sum(matmul(mixed_b, w_out).astype(jnp.bfloat16))
     grad_pieces = to_lanes(grad_picked)
+
+    attn_sum, grad_pieces = fence(attn_sum, grad_pieces)
     first_mine = jnp.concatenate(first_pieces)
     first_other = swap(first_mine)
-
-    attn_sum, first_other, grad_pieces = fence(attn_sum, first_other, grad_pieces)
     shared_pieces = to_lanes([shared_moved] * lanes)
     second_mine = jnp.concatenate(second_pieces)
     second_other = swap(second_mine)
@@ -1169,7 +1170,7 @@
     inverse_two = lax.rsqrt(jnp.mean(middle * middle, axis=-1, keepdims=True) + EPSILON)
     normed_two_b = (middle * inverse_two * gain_two).astype(jnp.bfloat16)
     x2 = gather(normed_two_b)
-    x2, shared_pieces, second_other = fence(x2, shared_pieces, second_other)
+    x2, shared_pieces, first_other, second_other = fence(x2, shared_pieces, first_other, second_other)
     x_pieces = to_lanes(picked(my_blocks(x2)))
     shared_w = by_lane(shared_pieces).transpose(1, 0, 2, 3).reshape(share * groups, 2 * hidden_n)
 
@@ -1177,18 +1178,33 @@
     shared_b = matmul(x2, shared_w[:, hidden_n:])
     shared_sig = jax.nn.sigmoid(shared_a)
     shared_hidden = (shared_a * shared_sig * shared_b).astype(jnp.bfloat16)
-    shared_part = matmul(shared_hidden, shared_out).astype(jnp.bfloat16)
     shared_up = matmul_nt(grad_all, shared_out)
     shared_ga = (shared_up * shared_b * shared_sig * (1.0 + shared_a * (1.0 - shared_sig))).astype(
         jnp.bfloat16
     )
     shared_gb = (shared_up * shared_a * shared_sig).astype(jnp.bfloat16)
     shared_g = jnp.concatenate([shared_ga, shared_gb], axis=1)
+    x_pieces[:3], shared_g, shared_hidden = fence(x_pieces[:3], shared_g, shared_hidden)
+    shared_part = matmul(shared_hidden, shared_out).astype(jnp.bfloat16)
     grad_shared_out = matmul_tn(shared_hidden, grad_all).astype(jnp.bfloat16)
     grad_shared_in = matmul_tn(x2, shared_g).astype(jnp.bfloat16)
     shared_back = matmul_nt(shared_g, shared_w).astype(jnp.bfloat16)
-    x_pieces, shared_part, shared_back, grad_shared_out, grad_shared_in = fence(
-        x_pieces, shared_part, shared_back, grad_shared_out, grad_shared_in
+    part = share // lanes
+    shared_in_lanes = grad_shared_in.reshape(groups, lanes, part, 2 * hidden_n)
+    shared_out_lanes = grad_shared_out.reshape(lanes, -1, 2 * hidden_n)
+    shared_sources = [
+        jnp.concatenate(
+            [
+                lax.dynamic_index_in_dim(shared_in_lanes, my_dp ^ step, 1, keepdims=False).reshape(
+                    groups * part, 2 * hidden_n
+                ),
+                lax.dynamic_index_in_dim(shared_out_lanes, my_dp ^ step, 0, keepdims=False),
+            ]
+        )
+        for step in range(lanes)
+    ]
+    x_pieces, shared_part, shared_back, shared_sources = fence(
+        x_pieces, shared_part, shared_back, shared_sources
     )
 
     def lane_parts(value):
@@ -1204,18 +1220,7 @@
         return sum(piece.astype(jnp.float32) for piece in pieces).astype(jnp.bfloat16)
 
     flat = (chips * capacity, D)
-    part = share // lanes
-    shared_parts = lane_exchange(
-        jnp.concatenate(
-            [
-                grad_shared_in.reshape(groups, lanes, part, 2 * hidden_n)
-                .transpose(1, 0, 2, 3)
-                .reshape(lanes, groups * part, 2 * hidden_n),
-                grad_shared_out.reshape(lanes, -1, 2 * hidden_n),
-            ],
-            axis=1,
-        )
-    )
+    shared_parts = to_lanes(shared_sources)
     router_lane = kv_cols - KVR
     spot = jnp.stack([my_dp, my_core, my_expert]).astype(jnp.int32)
     step_out = expert_step(
@@ -1239,23 +1244,20 @@
         logit_grad[:, :expert_count], ((0, 0), (router_lane, 128 - router_lane - expert_count))
     )
     grad_router = matmul_tn(x_rows, logit_wide)
+    back_pieces, grad_second, grad_router, result_b = fence(back_pieces, grad_second, grad_router, result_b)
+    result_sources, x_rows, grads, shared_parts = fence(split_rows(result_b), x_rows, grads, shared_parts)
+    result_pieces = to_lanes(result_sources)
     shared_sum = lane_sum(shared_parts)
-    back_pieces, grad_second, grad_router, result_b, x_rows, grads, shared_sum = fence(
-        back_pieces, grad_second, grad_router, result_b, x_rows, grads, shared_sum
-    )
-    shared_in_moved = exchange(shared_sum[: groups * part].reshape(groups, part, 2 * hidden_n))
-    shared_out_own = shared_sum[groups * part :].reshape(part, -1)
     grad_first_other = matmul_tn(x_rows, grads[1]).astype(jnp.bfloat16)
     grad_first_mine = matmul_tn(x_rows, grads[0]).astype(jnp.bfloat16)
 
-    result_pieces = to_lanes(split_rows(result_b))
     first_sent = swap(grad_first_other)
     second_hold, second_send = halves(grad_second, 0)
     second_sent = swap(second_send)
     back_part = add_mine(shared_back.astype(jnp.float32), placed(back_pieces)).astype(jnp.bfloat16)
     normed_two_grad = scatter_sum(back_part.reshape(length, D))
-    normed_two_grad, first_sent, second_sent, grad_first_mine = fence(
-        normed_two_grad, first_sent, second_sent, grad_first_mine
+    normed_two_grad, first_sent, second_sent, grad_first_mine, result_pieces[:3] = fence(
+        normed_two_grad, first_sent, second_sent, grad_first_mine, result_pieces[:3]
     )
     normed_two_grad = normed_two_grad.astype(jnp.float32)
     normal_two = middle * inverse_two
@@ -1265,13 +1267,61 @@
         scaled - normal_two * jnp.mean(scaled * normal_two, axis=-1, keepdims=True)
     )
     grad_first = (grad_first_mine.astype(jnp.float32) + first_sent.astype(jnp.float32)).astype(jnp.bfloat16)
-    first_back = lane_exchange(grad_first.reshape(lanes, D // lanes, half))
+    first_lanes = grad_first.reshape(lanes, D // lanes, half)
+    first_sources = [
+        lax.dynamic_index_in_dim(first_lanes, my_dp ^ step, 0, keepdims=False) for step in range(lanes)
+    ]
     grad_second = (second_hold.astype(jnp.float32) + second_sent.astype(jnp.float32)).astype(jnp.bfloat16)
 
     middle_all = gather(middle_grad.astype(jnp.bfloat16))
-    middle_all, result_pieces, grad_second, shared_in_moved = fence(
-        middle_all, result_pieces, grad_second, shared_in_moved
-    )
+    second_lanes = grad_second.reshape(half // 2, lanes, D // lanes)
+    second_sources = [
+        lax.dynamic_index_in_dim(second_lanes, my_dp ^ step, 1, keepdims=False) for step in range(lanes)
+    ]
+    first_back = to_lanes(first_sources)
+    middle_all, result_pieces, second_sources, first_back[:3], shared_sum = fence(
+        middle_all, result_pieces, second_sources, first_back[:3], shared_sum
+    )
+    shared_in_moved = exchange(shared_sum[: groups * part].reshape(groups, part, 2 * hidden_n))
+    shared_out_own = shared_sum[groups * part :].reshape(part, -1)
+    out_part = add_mine(shared_part.astype(jnp.float32), placed(result_pieces)).astype(jnp.bfloat16)
+    attn_grad = matmul_nt(middle_all, w_out).astype(jnp.bfloat16)
+    attn_grad, out_part = fence(attn_grad, out_part)
+    ffn = scatter_sum(out_part.reshape(length, D))
+    query_nope_grad, query_rope_grad, kv_up_grad, rope_grad = attend_back(
+        prefix, query, attn_grad, key_rope, kv_up, heads, scale
+    )
+    grad_out_w = matmul_tn(mixed_b, middle_all).astype(jnp.bfloat16)
+    out_w_parts = lane_rows(grad_out_w)
+
+    def own_slices(pieces, axis):
+        def of_core(core):
+            near = my_dp // 2 == core
+            pair = [jnp.where(near, pieces[i], pieces[2 + i]) for i in range(2)]
+            flip = my_dp % 2 == 1
+            return jnp.stack(
+                [jnp.where(flip, pair[1], pair[0]), jnp.where(flip, pair[0], pair[1])]
+            )
+
+        return ordered(of_core(my_core), swap(of_core(1 - my_core)), axis).astype(jnp.float32)
+
+    grad_kv_up = matmul_tn(latent_b, kv_up_grad).astype(jnp.bfloat16)
+    latent_up = matmul_nt(kv_up_grad, kv_up_w)
+    grad_kv_gain = jnp.sum(latent_up * latent_n, axis=0)
+    latent_scaled = latent_up * gain_kv
+    latent_grad = inverse_kv * (
+        latent_scaled - latent_n * jnp.mean(latent_scaled * latent_n, axis=-1, keepdims=True)
+    )
+    rope_grad = rotate(rope_grad, cosine, -sine_table)
+    kv_down_grad = jnp.concatenate([latent_grad, rope_grad], axis=1).astype(jnp.bfloat16)
+    query_rope_grad = rotate(
+        query_rope_grad.reshape(length, heads, DR), cosine[:, None, :], -sine_table[:, None, :]
+    )
+    query_grad = jnp.concatenate(
+        [query_nope_grad, query_rope_grad.reshape(length, heads * DR).astype(jnp.bfloat16)], axis=1
+    )
+    normed_part = matmul_nt(query_grad, query_w) + matmul_nt(kv_down_grad, kv_down_w)
+    grad_gain_one = jnp.sum(normed_part * (values_all * inverse_one), axis=0)
     early = jnp.concatenate(
         [
             shared_in_moved.reshape(groups, part, 2, hidden_n)
@@ -1281,50 +1331,6 @@
         ],
         axis=1,
     )
-    early_pieces = to_lanes([early] * lanes)
-    out_part = add_mine(shared_part.astype(jnp.float32), placed(result_pieces)).astype(jnp.bfloat16)
-    ffn = scatter_sum(out_part.reshape(length, D))
-    second_back = lane_exchange(
-        grad_second.reshape(half // 2, lanes, D // lanes).transpose(1, 0, 2)
-    )
-    attn_grad = matmul_nt(middle_all, w_out).astype(jnp.bfloat16)
-    query_nope_grad, query_rope_grad, kv_up_grad, rope_grad = attend_back(
-        prefix, query, attn_grad, key_rope, kv_up, heads, scale
-    )
-    query_nope_grad, query_rope_grad, kv_up_grad, rope_grad, first_back, early_pieces = fence(
-        query_nope_grad, query_rope_grad, kv_up_grad, rope_grad, first_back, early_pieces
-    )
-    grad_out_w = matmul_tn(mixed_b, middle_all).astype(jnp.bfloat16)
-    out_w_parts = lane_rows(grad_out_w)
-
-    def own_slices(pieces, axis):
-        def of_core(core):
-            near = my_dp // 2 == core
-            pair = [jnp.where(near, pieces[i], pieces[2 + i]) for i in range(2)]
-            flip = my_dp % 2 == 1
-            return jnp.stack(
-                [jnp.where(flip, pair[1], pair[0]), jnp.where(flip, pair[0], pair[1])]
-            )
-
-        return ordered(of_core(my_core), swap(of_core(1 - my_core)), axis).astype(jnp.float32)
-
-    grad_kv_up = matmul_tn(latent_b, kv_up_grad).astype(jnp.bfloat16)
-    latent_up = matmul_nt(kv_up_grad, kv_up_w)
-    grad_kv_gain = jnp.sum(latent_up * latent_n, axis=0)
-    latent_scaled = latent_up * gain_kv
-    latent_grad = inverse_kv * (
-        latent_scaled - latent_n * jnp.mean(latent_scaled * latent_n, axis=-1, keepdims=True)
-    )
-    rope_grad = rotate(rope_grad, cosine, -sine_table)
-    kv_down_grad = jnp.concatenate([latent_grad, rope_grad], axis=1).astype(jnp.bfloat16)
-    query_rope_grad = rotate(
-        query_rope_grad.reshape(length, heads, DR), cosine[:, None, :], -sine_table[:, None, :]
-    )
-    query_grad = jnp.concatenate(
-        [query_nope_grad, query_rope_grad.reshape(length, heads * DR).astype(jnp.bfloat16)], axis=1
-    )
-    normed_part = matmul_nt(query_grad, query_w) + matmul_nt(kv_down_grad, kv_down_w)
-    grad_gain_one = jnp.sum(normed_part * (values_all * inverse_one), axis=0)
     normed_part, ffn = fence(normed_part.astype(jnp.bfloat16), ffn)
     grad_query = matmul_tn(normed_b, query_grad).astype(jnp.bfloat16)
     attention_grad = jnp.concatenate(
@@ -1334,7 +1340,7 @@
         ],
         axis=2,
     ).reshape(groups * share, query_n + kv_width // fold)
-    attention_moved = exchange(lane_sum(lane_parts(attention_grad)))
+    attention_parts_sum = lane_parts(attention_grad)
 
     kv_wide = jnp.pad(kv_down_grad, ((0, 0), (0, 640 - kv_cols)))
     gains_grad = jnp.concatenate(
@@ -1352,8 +1358,13 @@
         matmul_tn(normed_b, kv_wide) + jnp.pad(grad_router + gains_wide, ((0, 0), (KVR, 0)))
     ).astype(jnp.bfloat16)
     small_sum = scatter_sum(small_grad)
-    small_sum, normed_part = fence(small_sum, normed_part)
     normed_grad = scatter_sum(normed_part)
+    normed_grad, first_back, attention_parts_sum, out_w_parts, early, second_sources = fence(
+        normed_grad, first_back, attention_parts_sum, out_w_parts, early, second_sources
+    )
+    attention_moved = exchange(lane_sum(attention_parts_sum))
+    early_pieces = to_lanes([early] * lanes)
+    second_back = to_lanes(second_sources)
     small_part = lane_sum(lane_rows(small_sum))
 
     grad_first = own_slices(first_back, 2)

time: 1040 us -> 956 us (0.919)
  waiting for transfers between devices: 447 us -> 354 us
    ppermute x45, waiting for transfers between devices: 364 us -> 286 us  [to_lane(): lax.ppermute(value, 'dp', [(lane, lane ^ step) for lane in range(lanes)])]
    reduce_scatter x5, waiting for transfers between devices: 22 us -> 47.8 us  [scatter_sum(): return lax.psum_scatter(value, group, scatter_dimension=0, tiled=True)]
    all_to_all x4, waiting for transfers between devices: 27.6 us -> 2.27 us  [exchange(): return lax.all_to_all(value, group, split_axis=0, concat_axis=0, tiled=True)]
    all_gather x5, waiting for transfers between devices: 16.8 us -> 2.11 us  [gather(): return lax.all_gather(value, group, axis=0, tiled=True)]
    unnamed x198 -> x314, local copies, waits for them, and re-layouts: 46 us -> 46.4 us
  transfers between devices with their start and end apart: 68 -> 68, of which waited for: 32 -> 27; matrix products, arithmetic and copies ran while one was open for 31% -> 36% of each run, Pallas kernels for 8% -> 8%
where the time goes in v2:
time: 956 us; the launch traced here: 947 us
  waiting for transfers between devices  354 us (37%)
  local copies, waits for them, and re-layouts  157 us (16%)
  matrix products  141 us (15%)
  other arithmetic  120 us (13%)
  Pallas kernels  79 us (8%)
  starting transfers between devices  78.4 us (8%)
  between operations  17.1 us (2%)
    ppermute x45, waiting for transfers between devices, to_lane(): lax.ppermute(value, 'dp', [(lane, lane ^ step) for lane in range(lanes)])  286 us
    dot_general x10, matrix products, matmul_tn(): lax.dot_general(left_side, right_side, (((0,), (0,)), ((), ())), preferre...  62 us
    pallas_call x1, Pallas kernels, expert_step(): pl.pallas_call(functools.partial(expert_kernel, expert_count), out_shape=...  60.7 us
    ppermute x45, starting transfers between devices, to_lane(): lax.ppermute(value, 'dp', [(lane, lane ^ step) for lane in range(lanes)])  57.9 us
    reduce_scatter x5, waiting for transfers between devices, scatter_sum(): return lax.psum_scatter(value, group, scatter_dimension=0, tiled=True)  47.8 us
    unnamed x314, local copies, waits for them, and re-layouts  46.4 us
    dot_general x8, matrix products, matmul(): return jnp.dot(left_side, right_side, preferred_element_type=jnp.float32)  32.8 us
    dot_general x6, matrix products, matmul_nt(): lax.dot_general(left_side, right_side, (((1,), (1,)), ((), ())), preferre...  27.1 us
  transfers between devices with their start and end apart: 68, of which 27 were waited for; matrix products, arithmetic and copies ran while one was open for 36% of the time, Pallas kernels for 8%

profile of v2, /device:TPU:0, one launch (start us, length us, event | category | flops | bytes accessed | tf_op | source)
XLA Modules:
  0.0 947.2 jit_solution(726636556294836831)
XLA Ops:
  34.5 11.2 %select_bitcast_fusion.4 = (bf16[512,1408]{1,0:T(8,128)(2,1)}, bf16[512,1408]{1,0:T(8,128)(2,1)}, bf16[512,1408]{1,0:T(8,128)(2,1)}, bf16[512,1408]{1,0:T(8,128)(2,1)}) fusion(bf16[2,512,1408]{2,1,0:T(8,128)(2,1)} %collective-permute-done.3, s32[]{:T(128)S(6)} %select_n.406, bf16[2,512,2816]{2,1,0:T(8,128)(2,1)} %param.30, s32[]{:T(128)S(6)} %select_n.407, ...), kind=kLoop, calls=%fused_computation.116 | loop fusion | flops 2883584 | bytes 17301544 | tf_op jit(solution)/shard_map/jit(_where)/select_n | solution.py:1065
  71.1 20.5 %collective-permute-done = bf16[8,64,512]{2,1,0:T(8,128)(2,1)S(1)} collective-permute-done((bf16[8,64,512]{2,1,0:T(8,128)(2,1)S(1)}, bf16[8,64,512]{2,1,0:T(8,128)(2,1)S(1)}, u32[]{:S(2)}, u32[]{:S(2)}) %collective-permute-start) | collective-permute-done | bytes 524320 | tf_op jit(solution)/shard_map/ppermute | solution.py:996
  94.0 9.8 %collective-permute-done.2 = bf16[8,64,512]{2,1,0:T(8,128)(2,1)S(1)} collective-permute-done((bf16[8,64,512]{2,1,0:T(8,128)(2,1)S(1)}, bf16[8,64,512]{2,1,0:T(8,128)(2,1)S(1)}, u32[]{:S(2)}, u32[]{:S(2)}) %collective-permute-start.2) | collective-permute-done | bytes 524320 | tf_op jit(solution)/shard_map/ppermute | solution.py:996
  163.5 14.5 %collective-permute-done.8 = bf16[704,512]{1,0:T(8,128)(2,1)} collective-permute-done((bf16[704,512]{1,0:T(8,128)(2,1)}, bf16[704,512]{1,0:T(8,128)(2,1)}, u32[]{:S(2)}, u32[]{:S(2)}) %collective-permute-start.8) | collective-permute-done | bytes 720928 | tf_op jit(solution)/shard_map/ppermute | solution.py:996
  193.4 23.3 %collective-permute-done.11 = bf16[4,72,2048]{2,1,0:T(8,128)(2,1)S(1)} collective-permute-done((bf16[4,72,2048]{2,1,0:T(8,128)(2,1)S(1)}, bf16[4,72,2048]{2,1,0:T(8,128)(2,1)S(1)}, u32[]{:S(2)}, u32[]{:S(2)}) %collective-permute-start.11) | collective-permute-done | bytes 1179680 | tf_op jit(solution)/shard_map/ppermute | solution.py:996
  216.7 25.5 %collective-permute-done.12 = bf16[4,72,2048]{2,1,0:T(8,128)(2,1)S(1)} collective-permute-done((bf16[4,72,2048]{2,1,0:T(8,128)(2,1)S(1)}, bf16[4,72,2048]{2,1,0:T(8,128)(2,1)S(1)}, u32[]{:S(2)}, u32[]{:S(2)}) %collective-permute-start.12) | collective-permute-done | bytes 1179680 | tf_op jit(solution)/shard_map/ppermute | solution.py:996
  275.3 8.7 collective-permute-done.14
  284.0 16.9 %collective-permute-done.16 = bf16[8,64,704]{2,1,0:T(8,128)(2,1)} collective-permute-done((bf16[8,64,704]{2,1,0:T(8,128)(2,1)}, bf16[8,64,704]{2,1,0:T(8,128)(2,1)}, u32[]{:S(2)}, u32[]{:S(2)}) %collective-permute-start.16) | collective-permute-done | bytes 720928 | tf_op jit(solution)/shard_map/ppermute | solution.py:996
  321.5 19.2 %collective-permute-done.20 = bf16[4,72,2048]{2,1,0:T(8,128)(2,1)S(1)} collective-permute-done((bf16[4,72,2048]{2,1,0:T(8,128)(2,1)S(1)}, bf16[4,72,2048]{2,1,0:T(8,128)(2,1)S(1)}, u32[]{:S(2)}, u32[]{:S(2)}) %collective-permute-start.20) | collective-permute-done | bytes 1179680 | tf_op jit(solution)/shard_map/ppermute | solution.py:996
  386.2 60.7 %expert_rows.1 = (bf16[288,2048]{1,0:T(8,128)(2,1)}, bf16[288,2048]{1,0:T(8,128)(2,1)}, bf16[288,2048]{1,0:T(8,128)(2,1)}, bf16[288,2048]{1,0:T(8,128)(2,1)}, bf...) custom-call(s32[3]{0:T(128)} %pad_add_fusion.spot, ...), custom_call_target="tpu_custom_call" | custom-call | flops 33218887680 | bytes 67928064 | tf_op jit(solution)/shard_map/expert_rows/pallas_call | solution.py:893
  450.5 13.4 %convolution_convert_fusion.3 = bf16[1408,2048]{1,0:T(8,128)(2,1)} fusion(bf16[1152,1408]{1,0:T(8,128)(2,1)} %get-tuple-element.220, bf16[1152,2048]{1,0:T(8,128)(2,1)} %get-tuple-element.221), kind=kOutput, calls=%fused_computation.16 | convolution fusion | flops 6646661120 | bytes 13729792 | tf_op jit(solution)/shard_map/dot_general | solution.py:60
  463.9 9.0 convolution_convert_fusion.2
  476.1 20.0 %collective-permute-done.26 = bf16[4,72,2048]{2,1,0:T(8,128)(2,1)S(1)} collective-permute-done((bf16[4,72,2048]{2,1,0:T(8,128)(2,1)}, bf16[4,72,2048]{2,1,0:T(8,128)(2,1)S(1)}, u32[]{:S(2)}, u32[]{:S(2)}) %collective-permute-start.26) | collective-permute-done | bytes 1179680 | tf_op jit(solution)/shard_map/ppermute | solution.py:996
  505.7 12.5 %convolution_convert_fusion.1 = bf16[2048,1408]{1,0:T(8,128)(2,1)S(1)} fusion(bf16[1152,2048]{1,0:T(8,128)(2,1)} %get-tuple-element.235, bf16[2,1152,1408]{2,1,0:T(8,128)(2,1)} %get-tuple-element.236), kind=kOutput, calls=%fused_computation.14 | convolution fusion | flops 6646661120 | bytes 13729792 | tf_op jit(solution)/shard_map/dot_general | solution.py:60
  521.3 10.3 %convolution_convert_fusion = bf16[2048,1408]{1,0:T(8,128)(2,1)} fusion(bf16[1152,2048]{1,0:T(8,128)(2,1)S(1)} %bitcast.347, bf16[2,1152,1408]{2,1,0:T(8,128)(2,1)S(1)} %bitcast.411), kind=kOutput, calls=%fused_computation.13 | convolution fusion | flops 6646661120 | bytes 13729792 | tf_op jit(solution)/shard_map/dot_general | solution.py:60
  531.6 15.7 %collective-permute-done.30 = bf16[4,72,2048]{2,1,0:T(8,128)(2,1)S(1)} collective-permute-done((bf16[4,72,2048]{2,1,0:T(8,128)(2,1)S(1)}, bf16[4,72,2048]{2,1,0:T(8,128)(2,1)S(1)}, u32[]{:S(2)}, u32[]{:S(2)}) %collective-permute-start.30) | collective-permute-done | bytes 1179680 | tf_op jit(solution)/shard_map/ppermute | solution.py:996
  596.9 27.2 %collective-permute-done.32 = bf16[4,72,2048]{2,1,0:T(8,128)(2,1)} collective-permute-done((bf16[4,72,2048]{2,1,0:T(8,128)(2,1)}, bf16[4,72,2048]{2,1,0:T(8,128)(2,1)}, u32[]{:S(2)}, u32[]{:S(2)}) %collective-permute-start.32) | collective-permute-done | bytes 1179680 | tf_op jit(solution)/shard_map/ppermute | solution.py:996
  638.6 11.9 %attend_back.1 = (bf16[1024,256]{1,0:T(8,128)(2,1)S(1)}, f32[1024,128]{1,0:T(8,128)S(1)}, bf16[1024,512]{1,0:T(8,128)(2,1)S(1)}, f32[1024,64]{1,0:T(8,128)S(1)}) custom-call(s32[1]{0:T(128)S(6)} %copy.423.prefix_ref, bf16[1024,384]{1,0:T(8,128)(2,1)S(1)} %copy-done.5, bf16[1024,256]{1,0:T(8,128)(2,1)S(1)} %copy-done.10, bf16[1024,64]{1,0:T(8,128)(2,1)S(1)} %copy-done.7, ...), custom_call_target="tpu_custom_call" | custom-call | flops 80530636800 | bytes 7077888 | tf_op jit(solution)/shard_map/attend_back/pallas_call | solution.py:713
  705.8 30.9 %reduce-scatter.14.cloned.1.call-done = bf16[256,640]{1,0:T(8,128)(2,1)} async-done(((bf16[2048,640]{1,0:T(8,128)(2,1)}), bf16[256,640]{1,0:T(8,128)(2,1)}) %reduce-scatter.14.cloned.1.call-update) | async-done | bytes 327696 | tf_op jit(solution)/shard_map/reduce_scatter | solution.py:971
  769.1 15.1 %collective-permute-done.37 = bf16[8,64,512]{2,1,0:T(8,128)(2,1)S(1)} collective-permute-done((bf16[8,64,512]{2,1,0:T(8,128)(2,1)}, bf16[8,64,512]{2,1,0:T(8,128)(2,1)S(1)}, u32[]{:S(2)}, u32[]{:S(2)}) %collective-permute-start.37) | collective-permute-done | bytes 524320 | tf_op jit(solution)/shard_map/ppermute | solution.py:996
  815.8 18.1 %collective-permute-done.49 = bf16[704,512]{1,0:T(8,128)(2,1)} collective-permute-done((bf16[704,512]{1,0:T(8,128)(2,1)}, bf16[704,512]{1,0:T(8,128)(2,1)}, u32[]{:S(2)}, u32[]{:S(2)}) %collective-permute-start.49) | collective-permute-done | bytes 720928 | tf_op jit(solution)/shard_map/ppermute | solution.py:996
  836.2 14.1 %collective-permute-done.50 = bf16[704,512]{1,0:T(8,128)(2,1)} collective-permute-done((bf16[704,512]{1,0:T(8,128)(2,1)}, bf16[704,512]{1,0:T(8,128)(2,1)}, u32[]{:S(2)}, u32[]{:S(2)}) %collective-permute-start.50) | collective-permute-done | bytes 720928 | tf_op jit(solution)/shard_map/ppermute | solution.py:996
  850.3 20.0 %collective-permute-done.51 = bf16[704,512]{1,0:T(8,128)(2,1)} collective-permute-done((bf16[704,512]{1,0:T(8,128)(2,1)}, bf16[704,512]{1,0:T(8,128)(2,1)}, u32[]{:S(2)}, u32[]{:S(2)}) %collective-permute-start.51) | collective-permute-done | bytes 720928 | tf_op jit(solution)/shard_map/ppermute | solution.py:996
  912.8 14.2 %all-gather.17.cloned.1.call-done = bf16[256,6784]{1,0:T(8,128)(2,1)} async-done(((bf16[64,6784]{1,0:T(8,128)(2,1)}), bf16[256,6784]{1,0:T(8,128)(2,1)}) %all-gather.17.cloned.1.call-update) | async-done | bytes 3473424 | tf_op jit(solution)/shard_map/all_gather | solution.py:1373
  (654 shorter events, 487.5 us)
Async XLA Ops:
  7.2 97.4 %all-gather.9.cloned.1.call-start = ((), (), s32[]{:S(2)}) async-start(), calls=%async_computation.10 | async-start | bytes 2949120 | tf_op jit(solution)/shard_map/all_gather | solution.py:968
  11.8 94.9 %all-gather.7.cloned.1.call-start = ((), (), s32[]{:S(2)}) async-start(), calls=%async_computation.9 | async-start | bytes 4718592 | tf_op jit(solution)/shard_map/all_gather | solution.py:968
  33.5 149.4 %all-gather.11.cloned.1.call-start = ((), (), s32[]{:S(2)}) async-start(), calls=%async_computation.12 | async-start | bytes 4718592 | tf_op jit(solution)/shard_map/all_gather | solution.py:968
  45.7 58.9 %collective-permute-start.4 = (bf16[512,1408]{1,0:T(8,128)(2,1)}, bf16[512,1408]{1,0:T(8,128)(2,1)S(1)}, u32[]{:S(2)}, u32[]{:S(2)}) collective-permute-start(bf16[512,1408]{1,0:T(8,128)(2,1)} %get-tuple-element.401), channel_id=1, source_target_pairs={{0,8},{8,0},{16,24},{24,16},{1,9},{9,1},{17,25},{25,17},{2,10},{10... | collective-permute-start | bytes 4325384 | tf_op jit(solution)/shard_map/ppermute | solution.py:996
  69.6 87.2 %collective-permute-start.6 = (bf16[512,1408]{1,0:T(8,128)(2,1)}, bf16[512,1408]{1,0:T(8,128)(2,1)}, u32[]{:S(2)}, u32[]{:S(2)}) collective-permute-start(bf16[512,1408]{1,0:T(8,128)(2,1)} %get-tuple-element.400), channel_id=1, source_target_pairs={{0,16},{8,24},{16,0},{24,8},{1,17},{9,25},{17,1},{25,9},{2,18},{10... | collective-permute-start | bytes 4325384 | tf_op jit(solution)/shard_map/ppermute | solution.py:996
  91.5 65.3 %collective-permute-start.7 = (bf16[512,1408]{1,0:T(8,128)(2,1)}, bf16[512,1408]{1,0:T(8,128)(2,1)}, u32[]{:S(2)}, u32[]{:S(2)}) collective-permute-start(bf16[512,1408]{1,0:T(8,128)(2,1)} %get-tuple-element.399), channel_id=1, source_target_pairs={{0,24},{8,16},{16,8},{24,0},{1,25},{9,17},{17,9},{25,1},{2,26},{10... | collective-permute-start | bytes 4325384 | tf_op jit(solution)/shard_map/ppermute | solution.py:996
  142.6 100.6 %reduce-scatter.6.cloned.1.call-start = ((), (), s32[]{:S(2)}) async-start(), calls=%async_computation.11 | async-start | bytes 4718592 | tf_op jit(solution)/shard_map/reduce_scatter | solution.py:971
  181.3 119.7 %all-gather.13.cloned.1.call-start = ((), (), s32[]{:S(2)}) async-start(), calls=%async_computation.13 | async-start | bytes 4718592 | tf_op jit(solution)/shard_map/all_gather | solution.py:968
  247.1 304.4 %reduce-scatter.8.cloned.1.call-start = ((), (), s32[]{:S(2)}) async-start(), calls=%async_computation.14 | async-start | bytes 4718592 | tf_op jit(solution)/shard_map/reduce_scatter | solution.py:971
  315.1 62.5 %collective-permute-start.21 = (bf16[4,72,2048]{2,1,0:T(8,128)(2,1)}, bf16[4,72,2048]{2,1,0:T(8,128)(2,1)}, u32[]{:S(2)}, u32[]{:S(2)}) collective-permute-start(bf16[4,72,2048]{2,1,0:T(8,128)(2,1)} %convolution_convert_fusion.10), channel_id=1, source_target_pairs={{0,24},{8,16},{16,8},{24,0},{1,25},{9,17},{17,9},{25,1},{2,26},{10... | collective-permute-start | bytes 3538952 | tf_op jit(solution)/shard_map/ppermute | solution.py:996
  380.0 66.9 %collective-permute-start.22 = (bf16[768,704]{0,1:T(8,128)(2,1)}, bf16[768,704]{0,1:T(8,128)(2,1)}, u32[]{:S(2)}, u32[]{:S(2)}) collective-permute-start(bf16[768,704]{0,1:T(8,128)(2,1)} %copy.351), channel_id=1, source_target_pairs={{0,8},{8,0},{16,24},{24,16},{1,9},{9,1},{17,25},{25,17},{2,10},{10... | collective-permute-start | bytes 3244040 | tf_op jit(solution)/shard_map/ppermute | solution.py:996
  382.9 64.1 %collective-permute-start.23 = (bf16[768,704]{0,1:T(8,128)(2,1)}, bf16[768,704]{0,1:T(8,128)(2,1)S(1)}, u32[]{:S(2)}, u32[]{:S(2)}) collective-permute-start(bf16[768,704]{0,1:T(8,128)(2,1)} %copy.352), channel_id=1, source_target_pairs={{0,16},{8,24},{16,0},{24,8},{1,17},{9,25},{17,1},{25,9},{2,18},{10... | collective-permute-start | bytes 3244040 | tf_op jit(solution)/shard_map/ppermute | solution.py:996
  384.8 62.1 %collective-permute-start.24 = (bf16[768,704]{0,1:T(8,128)(2,1)}, bf16[768,704]{0,1:T(8,128)(2,1)S(1)}, u32[]{:S(2)}, u32[]{:S(2)}) collective-permute-start(bf16[768,704]{0,1:T(8,128)(2,1)} %copy.353), channel_id=1, source_target_pairs={{0,24},{8,16},{16,8},{24,0},{1,25},{9,17},{17,9},{25,1},{2,26},{10... | collective-permute-start | bytes 3244040 | tf_op jit(solution)/shard_map/ppermute | solution.py:996
  501.2 123.0 %all-gather.15.cloned.1.call-start = ((), (), s32[]{:S(2)}) async-start(), calls=%async_computation.15 | async-start | bytes 4718592 | tf_op jit(solution)/shard_map/all_gather | solution.py:968
  555.4 130.0 %reduce-scatter.10.cloned.1.call-start = ((), (), s32[]{:S(2)}) async-start(), calls=%async_computation.16 | async-start | bytes 4718592 | tf_op jit(solution)/shard_map/reduce_scatter | solution.py:971
  563.9 60.3 %collective-permute-start.33 = (bf16[512,1408]{1,0:T(8,128)(2,1)}, bf16[512,1408]{1,0:T(8,128)(2,1)}, u32[]{:S(2)}, u32[]{:S(2)}) collective-permute-start(bf16[512,1408]{1,0:T(8,128)(2,1)} %get-tuple-element.411), channel_id=1, source_target_pairs={{0,8},{8,0},{16,24},{24,16},{1,9},{9,1},{17,25},{25,17},{2,10},{10... | collective-permute-start | bytes 4325384 | tf_op jit(solution)/shard_map/ppermute | solution.py:996
  635.2 101.5 %reduce-scatter.14.cloned.1.call-start = ((), (), s32[]{:S(2)}) async-start(), calls=%async_computation.18 | async-start | bytes 2949120 | tf_op jit(solution)/shard_map/reduce_scatter | solution.py:971
  677.4 114.1 %reduce-scatter.12.cloned.1.call-start = ((), (), s32[]{:S(2)}) async-start(), calls=%async_computation.17 | async-start | bytes 4718592 | tf_op jit(solution)/shard_map/reduce_scatter | solution.py:971
  685.5 61.5 %collective-permute-start.35 = (bf16[512,1408]{1,0:T(8,128)(2,1)}, bf16[512,1408]{1,0:T(8,128)(2,1)}, u32[]{:S(2)}, u32[]{:S(2)}) collective-permute-start(bf16[512,1408]{1,0:T(8,128)(2,1)} %get-tuple-element.409), channel_id=1, source_target_pairs={{0,24},{8,16},{16,8},{24,0},{1,25},{9,17},{17,9},{25,1},{2,26},{10... | collective-permute-start | bytes 4325384 | tf_op jit(solution)/shard_map/ppermute | solution.py:996
  791.5 93.6 %collective-permute-start.45 = (bf16[64,8448]{1,0:T(8,128)(2,1)S(1)}, bf16[64,8448]{1,0:T(8,128)(2,1)}, u32[]{:S(2)}, u32[]{:S(2)}) collective-permute-start(bf16[64,8448]{1,0:T(8,128)(2,1)S(1)} %pad_maximum_fusion.8), channel_id=1, source_target_pairs={{0,8},{8,0},{16,24},{24,16},{1,9},{9,1},{17,25},{25,17},{2,10},{10... | collective-permute-start | bytes 3244040 | tf_op jit(solution)/shard_map/ppermute | solution.py:996
  793.0 94.3 %collective-permute-start.46 = (bf16[64,8448]{1,0:T(8,128)(2,1)S(1)}, bf16[64,8448]{1,0:T(8,128)(2,1)}, u32[]{:S(2)}, u32[]{:S(2)}) collective-permute-start(bf16[64,8448]{1,0:T(8,128)(2,1)S(1)} %pad_maximum_fusion.8), channel_id=1, source_target_pairs={{0,16},{8,24},{16,0},{24,8},{1,17},{9,25},{17,1},{25,9},{2,18},{10... | collective-permute-start | bytes 3244040 | tf_op jit(solution)/shard_map/ppermute | solution.py:996
  796.5 73.9 %collective-permute-start.51 = (bf16[704,512]{1,0:T(8,128)(2,1)}, bf16[704,512]{1,0:T(8,128)(2,1)}, u32[]{:S(2)}, u32[]{:S(2)}) collective-permute-start(bf16[704,512]{1,0:T(8,128)(2,1)} %bitcast.317), channel_id=1, source_target_pairs={{0,16},{8,24},{16,0},{24,8},{1,17},{9,25},{17,1},{25,9},{2,18},{10... | collective-permute-start | bytes 2162696 | tf_op jit(solution)/shard_map/ppermute | solution.py:996
  803.7 70.8 %all-to-all-start.3 = ((bf16[8,64,512]{2,1,0:T(8,128)(2,1)}), bf16[8,64,512]{2,1,0:T(8,128)(2,1)S(1)}, u32[]{:S(2)}, u32[]{:S(2)}) async-start(bf16[8,64,512]{2,1,0:T(8,128)(2,1)} %add_convert_fusion.4), calls=%async_computation.7 | async-start | bytes 1048576 | tf_op jit(solution)/shard_map/all_to_all | solution.py:993
  807.3 119.8 %all-gather.17.cloned.1.call-start = ((), (), s32[]{:S(2)}) async-start(), calls=%async_computation.19 | async-start | bytes 4341760 | tf_op jit(solution)/shard_map/all_gather | solution.py:1373
  (192 other events, 3144.2 us)
Sparse Core Ops, SparseCore 0:
  11.9 46.9 all-gather.8
  60.5 46.0 all-gather.6
  108.3 51.9 all-gather.10
  181.4 51.0 reduce-scatter.5
  247.2 47.3 all-gather.12
  501.3 50.1 reduce-scatter.7
  555.5 48.1 all-gather.14
  635.3 50.0 reduce-scatter.9
  688.3 48.3 reduce-scatter.13
  739.4 52.0 reduce-scatter.11
  880.5 46.4 all-gather.16

commit v3 on v2

--- a/solution.py
+++ b/solution.py
@@ -1363,7 +1363,7 @@
         normed_grad, first_back, attention_parts_sum, out_w_parts, early, second_sources
     )
     attention_moved = exchange(lane_sum(attention_parts_sum))
-    early_pieces = to_lanes([early] * lanes)
+    early = lax.all_gather(early, "dp", axis=0, tiled=True)
     second_back = to_lanes(second_sources)
     small_part = lane_sum(lane_rows(small_sum))
 
@@ -1372,10 +1372,6 @@
     def lane_gather(value):
         return lax.all_gather(value, "dp", axis=0, tiled=True)
 
-    early = by_lane(early_pieces).reshape(share, -1)
-    cut = 2 * groups * hidden_n
-    shared_in_grad = early[:, :cut].astype(jnp.float32)
-    shared_out_grad = early[:, cut:].reshape(hidden_n, D).astype(jnp.float32)
     query_cols = attention_moved[..., :query_n].transpose(1, 0, 2)
     query_cols = jnp.concatenate(
         [
@@ -1391,8 +1387,11 @@
         .reshape(part, groups * kv_width // fold)
     )
     late = jnp.concatenate([query_cols, kv_cols_grad, lane_sum(out_w_parts), small_part], axis=1)
-    late, normed_grad = fence(late, normed_grad)
+    late, normed_grad, early = fence(late, normed_grad, early)
     late = lane_gather(late)
+    cut = 2 * groups * hidden_n
+    shared_in_grad = early[:, :cut].astype(jnp.float32)
+    shared_out_grad = early[:, cut:].reshape(hidden_n, D).astype(jnp.float32)
     cut = H * (DN + DR)
     query_grad_out = late[:, :cut].astype(jnp.float32)
     kv_up_grad_out = (

time: 956 us -> 953 us (level)
  waiting for transfers between devices: 354 us -> 364 us
    all_to_all x4, waiting for transfers between devices: 2.27 us -> 18.6 us  [exchange(): return lax.all_to_all(value, group, split_axis=0, concat_axis=0, tiled=True)]
    ppermute x45 -> x42, waiting for transfers between devices: 286 us -> 276 us  [to_lane(): lax.ppermute(value, 'dp', [(lane, lane ^ step) for lane in range(lanes)])]
    dynamic_update_slice x12 -> x8, local copies, waits for them, and re-layouts: 14 us -> 3.89 us  [by_lane(): full = lax.dynamic_update_index_in_dim(full, pieces[step], my_dp ^ step, 0)]
    ppermute x45 -> x42, starting transfers between devices: 57.9 us -> 51.2 us  [to_lane(): lax.ppermute(value, 'dp', [(lane, lane ^ step) for lane in range(lanes)])]
    unnamed x314 -> x296, local copies, waits for them, and re-layouts: 46.4 us -> 46.9 us
  transfers between devices with their start and end apart: 68 -> 66, of which waited for: 27 -> 29; matrix products, arithmetic and copies ran while one was open for 36% -> 36% of each run, Pallas kernels for 8% -> 8%
where the time goes in v3:
time: 953 us; the launch traced here: 942 us
  waiting for transfers between devices  364 us (38%)
  local copies, waits for them, and re-layouts  153 us (16%)
  matrix products  140 us (15%)
  other arithmetic  118 us (12%)
  Pallas kernels  79 us (8%)
  starting transfers between devices  71.8 us (8%)
  between operations  17.6 us (2%)
    ppermute x42, waiting for transfers between devices, to_lane(): lax.ppermute(value, 'dp', [(lane, lane ^ step) for lane in range(lanes)])  276 us
    dot_general x10, matrix products, matmul_tn(): lax.dot_general(left_side, right_side, (((0,), (0,)), ((), ())), preferre...  62.5 us
    pallas_call x1, Pallas kernels, expert_step(): pl.pallas_call(functools.partial(expert_kernel, expert_count), out_shape=...  60.9 us
    ppermute x42, starting transfers between devices, to_lane(): lax.ppermute(value, 'dp', [(lane, lane ^ step) for lane in range(lanes)])  51.2 us
    unnamed x296, local copies, waits for them, and re-layouts  46.9 us
    reduce_scatter x5, waiting for transfers between devices, scatter_sum(): return lax.psum_scatter(value, group, scatter_dimension=0, tiled=True)  45.3 us
    dot_general x8, matrix products, matmul(): return jnp.dot(left_side, right_side, preferred_element_type=jnp.float32)  31.4 us
    dot_general x6, matrix products, matmul_nt(): lax.dot_general(left_side, right_side, (((1,), (1,)), ((), ())), preferre...  26.8 us
  transfers between devices with their start and end apart: 66, of which 29 were waited for; matrix products, arithmetic and copies ran while one was open for 36% of the time, Pallas kernels for 8%

profile of v3, /device:TPU:0, one launch (start us, length us, event | category | flops | bytes accessed | tf_op | source)
XLA Modules:
  0.0 942.3 jit_solution(5841610822037375050)
XLA Ops:
  35.2 11.2 %select_bitcast_fusion.4 = (bf16[512,1408]{1,0:T(8,128)(2,1)}, bf16[512,1408]{1,0:T(8,128)(2,1)}, bf16[512,1408]{1,0:T(8,128)(2,1)}, bf16[512,1408]{1,0:T(8,128)(2,1)}) fusion(bf16[2,512,1408]{2,1,0:T(8,128)(2,1)} %collective-permute-done.3, s32[]{:T(128)S(6)} %select_n.401, bf16[2,512,2816]{2,1,0:T(8,128)(2,1)} %param.30, s32[]{:T(128)S(6)} %select_n.402, ...), kind=kLoop, calls=%fused_computation.116 | loop fusion | flops 2883584 | bytes 17301544 | tf_op jit(solution)/shard_map/jit(_where)/select_n | solution.py:1065
  71.5 21.7 %collective-permute-done.2 = bf16[8,64,512]{2,1,0:T(8,128)(2,1)S(1)} collective-permute-done((bf16[8,64,512]{2,1,0:T(8,128)(2,1)S(1)}, bf16[8,64,512]{2,1,0:T(8,128)(2,1)S(1)}, u32[]{:S(2)}, u32[]{:S(2)}) %collective-permute-start.2) | collective-permute-done | bytes 524320 | tf_op jit(solution)/shard_map/ppermute | solution.py:996
  93.7 9.8 %collective-permute-done = bf16[8,64,512]{2,1,0:T(8,128)(2,1)S(1)} collective-permute-done((bf16[8,64,512]{2,1,0:T(8,128)(2,1)S(1)}, bf16[8,64,512]{2,1,0:T(8,128)(2,1)S(1)}, u32[]{:S(2)}, u32[]{:S(2)}) %collective-permute-start) | collective-permute-done | bytes 524320 | tf_op jit(solution)/shard_map/ppermute | solution.py:996
  159.4 15.0 %collective-permute-done.6 = bf16[512,1408]{1,0:T(8,128)(2,1)} collective-permute-done((bf16[512,1408]{1,0:T(8,128)(2,1)}, bf16[512,1408]{1,0:T(8,128)(2,1)}, u32[]{:S(2)}, u32[]{:S(2)}) %collective-permute-start.6) | collective-permute-done | bytes 1441824 | tf_op jit(solution)/shard_map/ppermute | solution.py:996
  203.2 23.3 %collective-permute-done.11 = bf16[4,72,2048]{2,1,0:T(8,128)(2,1)S(1)} collective-permute-done((bf16[4,72,2048]{2,1,0:T(8,128)(2,1)S(1)}, bf16[4,72,2048]{2,1,0:T(8,128)(2,1)S(1)}, u32[]{:S(2)}, u32[]{:S(2)}) %collective-permute-start.11) | collective-permute-done | bytes 1179680 | tf_op jit(solution)/shard_map/ppermute | solution.py:996
  226.6 23.5 %collective-permute-done.12 = bf16[4,72,2048]{2,1,0:T(8,128)(2,1)S(1)} collective-permute-done((bf16[4,72,2048]{2,1,0:T(8,128)(2,1)S(1)}, bf16[4,72,2048]{2,1,0:T(8,128)(2,1)S(1)}, u32[]{:S(2)}, u32[]{:S(2)}) %collective-permute-start.12) | collective-permute-done | bytes 1179680 | tf_op jit(solution)/shard_map/ppermute | solution.py:996
  283.1 9.7 %collective-permute-done.16 = bf16[8,64,704]{2,1,0:T(8,128)(2,1)S(1)} collective-permute-done((bf16[8,64,704]{2,1,0:T(8,128)(2,1)}, bf16[8,64,704]{2,1,0:T(8,128)(2,1)S(1)}, u32[]{:S(2)}, u32[]{:S(2)}) %collective-permute-start.16) | collective-permute-done | bytes 720928 | tf_op jit(solution)/shard_map/ppermute | solution.py:996
  292.7 15.1 %collective-permute-done.15 = bf16[8,64,704]{2,1,0:T(8,128)(2,1)} collective-permute-done((bf16[8,64,704]{2,1,0:T(8,128)(2,1)}, bf16[8,64,704]{2,1,0:T(8,128)(2,1)}, u32[]{:S(2)}, u32[]{:S(2)}) %collective-permute-start.15) | collective-permute-done | bytes 720928 | tf_op jit(solution)/shard_map/ppermute | solution.py:996
  328.4 14.3 %collective-permute-done.19 = bf16[4,72,2048]{2,1,0:T(8,128)(2,1)S(1)} collective-permute-done((bf16[4,72,2048]{2,1,0:T(8,128)(2,1)S(1)}, bf16[4,72,2048]{2,1,0:T(8,128)(2,1)S(1)}, u32[]{:S(2)}, u32[]{:S(2)}) %collective-permute-start.19) | collective-permute-done | bytes 1179680 | tf_op jit(solution)/shard_map/ppermute | solution.py:996
  342.7 25.3 %collective-permute-done.20 = bf16[4,72,2048]{2,1,0:T(8,128)(2,1)S(1)} collective-permute-done((bf16[4,72,2048]{2,1,0:T(8,128)(2,1)S(1)}, bf16[4,72,2048]{2,1,0:T(8,128)(2,1)S(1)}, u32[]{:S(2)}, u32[]{:S(2)}) %collective-permute-start.20) | collective-permute-done | bytes 1179680 | tf_op jit(solution)/shard_map/ppermute | solution.py:996
  408.3 60.9 %expert_rows.1 = (bf16[288,2048]{1,0:T(8,128)(2,1)}, bf16[288,2048]{1,0:T(8,128)(2,1)}, bf16[288,2048]{1,0:T(8,128)(2,1)}, bf16[288,2048]{1,0:T(8,128)(2,1)}, bf...) custom-call(s32[3]{0:T(128)} %pad_add_fusion.spot, ...), custom_call_target="tpu_custom_call" | custom-call | flops 33218887680 | bytes 67928064 | tf_op jit(solution)/shard_map/expert_rows/pallas_call | solution.py:893
  472.8 13.1 %convolution_convert_fusion.3 = bf16[1408,2048]{1,0:T(8,128)(2,1)} fusion(bf16[1152,1408]{1,0:T(8,128)(2,1)} %get-tuple-element.221, bf16[1152,2048]{1,0:T(8,128)(2,1)} %get-tuple-element.222), kind=kOutput, calls=%fused_computation.16 | convolution fusion | flops 6646661120 | bytes 13729792 | tf_op jit(solution)/shard_map/dot_general | solution.py:60
  485.9 9.0 convolution_convert_fusion.2
  508.2 12.3 %convolution_convert_fusion.1 = bf16[2048,1408]{1,0:T(8,128)(2,1)S(1)} fusion(bf16[1152,2048]{1,0:T(8,128)(2,1)} %get-tuple-element.236, bf16[2,1152,1408]{2,1,0:T(8,128)(2,1)} %get-tuple-element.237), kind=kOutput, calls=%fused_computation.14 | convolution fusion | flops 6646661120 | bytes 13729792 | tf_op jit(solution)/shard_map/dot_general | solution.py:60
  524.0 10.2 %convolution_convert_fusion = bf16[2048,1408]{1,0:T(8,128)(2,1)} fusion(bf16[1152,2048]{1,0:T(8,128)(2,1)S(1)} %bitcast.338, bf16[2,1152,1408]{2,1,0:T(8,128)(2,1)S(1)} %bitcast.405), kind=kOutput, calls=%fused_computation.13 | convolution fusion | flops 6646661120 | bytes 13729792 | tf_op jit(solution)/shard_map/dot_general | solution.py:60
  534.3 15.3 %collective-permute-done.30 = bf16[4,72,2048]{2,1,0:T(8,128)(2,1)S(1)} collective-permute-done((bf16[4,72,2048]{2,1,0:T(8,128)(2,1)S(1)}, bf16[4,72,2048]{2,1,0:T(8,128)(2,1)S(1)}, u32[]{:S(2)}, u32[]{:S(2)}) %collective-permute-start.30) | collective-permute-done | bytes 1179680 | tf_op jit(solution)/shard_map/ppermute | solution.py:996
  599.0 27.2 %collective-permute-done.32 = bf16[4,72,2048]{2,1,0:T(8,128)(2,1)} collective-permute-done((bf16[4,72,2048]{2,1,0:T(8,128)(2,1)}, bf16[4,72,2048]{2,1,0:T(8,128)(2,1)}, u32[]{:S(2)}, u32[]{:S(2)}) %collective-permute-start.32) | collective-permute-done | bytes 1179680 | tf_op jit(solution)/shard_map/ppermute | solution.py:996
  638.9 11.7 %attend_back.1 = (bf16[1024,256]{1,0:T(8,128)(2,1)S(1)}, f32[1024,128]{1,0:T(8,128)S(1)}, bf16[1024,512]{1,0:T(8,128)(2,1)S(1)}, f32[1024,64]{1,0:T(8,128)S(1)}) custom-call(s32[1]{0:T(128)S(6)} %copy.419.prefix_ref, bf16[1024,384]{1,0:T(8,128)(2,1)S(1)} %copy-done.5, bf16[1024,256]{1,0:T(8,128)(2,1)S(1)} %convolution_convert_fusion.21.grad_ref, ...), custom_call_target="tpu_custom_call" | custom-call | flops 80530636800 | bytes 7077888 | tf_op jit(solution)/shard_map/attend_back/pallas_call | solution.py:713
  672.1 13.4 %reduce-scatter.10.cloned.1.call-done = bf16[128,2048]{1,0:T(8,128)(2,1)} async-done(((bf16[1024,2048]{1,0:T(8,128)(2,1)}), bf16[128,2048]{1,0:T(8,128)(2,1)}) %reduce-scatter.10.cloned.1.call-update) | async-done | bytes 524304 | tf_op jit(solution)/shard_map/reduce_scatter | solution.py:971
  722.2 16.9 %all-to-all-done.2 = bf16[8,64,704]{2,1,0:T(8,128)(2,1)S(1)} async-done(((bf16[8,64,704]{2,1,0:T(8,128)(2,1)}), bf16[8,64,704]{2,1,0:T(8,128)(2,1)S(1)}, u32[]{:S(2)}, u32[]{:S(2)}) %all-to-all-start.2) | async-done | bytes 720928 | tf_op jit(solution)/shard_map/all_to_all | solution.py:993
  760.9 31.2 %reduce-scatter.14.cloned.1.call-done = bf16[256,640]{1,0:T(8,128)(2,1)} async-done(((bf16[2048,640]{1,0:T(8,128)(2,1)}), bf16[256,640]{1,0:T(8,128)(2,1)}) %reduce-scatter.14.cloned.1.call-update) | async-done | bytes 327696 | tf_op jit(solution)/shard_map/reduce_scatter | solution.py:971
  820.1 15.0 %collective-permute-done.46 = bf16[704,512]{1,0:T(8,128)(2,1)S(1)} collective-permute-done((bf16[704,512]{1,0:T(8,128)(2,1)}, bf16[704,512]{1,0:T(8,128)(2,1)S(1)}, u32[]{:S(2)}, u32[]{:S(2)}) %collective-permute-start.46) | collective-permute-done | bytes 720928 | tf_op jit(solution)/shard_map/ppermute | solution.py:996
  835.1 31.6 %collective-permute-done.47 = bf16[704,512]{1,0:T(8,128)(2,1)S(1)} collective-permute-done((bf16[704,512]{1,0:T(8,128)(2,1)}, bf16[704,512]{1,0:T(8,128)(2,1)S(1)}, u32[]{:S(2)}, u32[]{:S(2)}) %collective-permute-start.47) | collective-permute-done | bytes 720928 | tf_op jit(solution)/shard_map/ppermute | solution.py:996
  901.2 20.3 %all-gather.20.cloned.1.call-done = bf16[256,6784]{1,0:T(8,128)(2,1)} async-done(((bf16[64,6784]{1,0:T(8,128)(2,1)}), bf16[256,6784]{1,0:T(8,128)(2,1)}) %all-gather.20.cloned.1.call-update) | async-done | bytes 3473424 | tf_op jit(solution)/shard_map/all_gather | solution.py:1373
  (627 shorter events, 467.8 us)
Async XLA Ops:
  7.2 97.1 %all-gather.10.cloned.1.call-start = ((), (), s32[]{:S(2)}) async-start(), calls=%async_computation.10 | async-start | bytes 2949120 | tf_op jit(solution)/shard_map/all_gather | solution.py:968
  11.8 94.5 %all-gather.8.cloned.1.call-start = ((), (), s32[]{:S(2)}) async-start(), calls=%async_computation.9 | async-start | bytes 4718592 | tf_op jit(solution)/shard_map/all_gather | solution.py:968
  34.2 158.5 %all-gather.12.cloned.1.call-start = ((), (), s32[]{:S(2)}) async-start(), calls=%async_computation.12 | async-start | bytes 4718592 | tf_op jit(solution)/shard_map/all_gather | solution.py:968
  69.1 90.2 %collective-permute-start.7 = (bf16[512,1408]{1,0:T(8,128)(2,1)}, bf16[512,1408]{1,0:T(8,128)(2,1)}, u32[]{:S(2)}, u32[]{:S(2)}) collective-permute-start(bf16[512,1408]{1,0:T(8,128)(2,1)} %get-tuple-element.401), channel_id=1, source_target_pairs={{0,24},{8,16},{16,8},{24,0},{1,25},{9,17},{17,9},{25,1},{2,26},{10... | collective-permute-start | bytes 4325384 | tf_op jit(solution)/shard_map/ppermute | solution.py:996
  93.2 81.2 %collective-permute-start.6 = (bf16[512,1408]{1,0:T(8,128)(2,1)}, bf16[512,1408]{1,0:T(8,128)(2,1)}, u32[]{:S(2)}, u32[]{:S(2)}) collective-permute-start(bf16[512,1408]{1,0:T(8,128)(2,1)} %get-tuple-element.402), channel_id=1, source_target_pairs={{0,16},{8,24},{16,0},{24,8},{1,17},{9,25},{17,1},{25,9},{2,18},{10... | collective-permute-start | bytes 4325384 | tf_op jit(solution)/shard_map/ppermute | solution.py:996
  110.9 70.2 %collective-permute-start.8 = (bf16[704,512]{1,0:T(8,128)(2,1)}, bf16[704,512]{1,0:T(8,128)(2,1)}, u32[]{:S(2)}, u32[]{:S(2)}) collective-permute-start(bf16[704,512]{1,0:T(8,128)(2,1)} %get-tuple-element.168), channel_id=1, source_target_pairs={{0,8},{8,0},{16,24},{24,16},{1,9},{9,1},{17,25},{25,17},{2,10},{10... | collective-permute-start | bytes 2162696 | tf_op jit(solution)/shard_map/ppermute | solution.py:996
  112.3 75.5 %collective-permute-start.9 = (bf16[704,512]{1,0:T(8,128)(2,1)}, bf16[704,512]{1,0:T(8,128)(2,1)}, u32[]{:S(2)}, u32[]{:S(2)}) collective-permute-start(bf16[704,512]{1,0:T(8,128)(2,1)} %get-tuple-element.169), channel_id=1, source_target_pairs={{0,16},{8,24},{16,0},{24,8},{1,17},{9,25},{17,1},{25,9},{2,18},{10... | collective-permute-start | bytes 2162696 | tf_op jit(solution)/shard_map/ppermute | solution.py:996
  113.8 74.0 %collective-permute-start.10 = (bf16[704,512]{1,0:T(8,128)(2,1)}, bf16[704,512]{1,0:T(8,128)(2,1)}, u32[]{:S(2)}, u32[]{:S(2)}) collective-permute-start(bf16[704,512]{1,0:T(8,128)(2,1)} %get-tuple-element.170), channel_id=1, source_target_pairs={{0,24},{8,16},{16,8},{24,0},{1,25},{9,17},{17,9},{25,1},{2,26},{10... | collective-permute-start | bytes 2162696 | tf_op jit(solution)/shard_map/ppermute | solution.py:996
  117.0 70.8 %all-to-all-start.1 = ((bf16[8,64,704]{2,1,0:T(8,128)(2,1)}), bf16[8,64,704]{2,1,0:T(8,128)(2,1)}, u32[]{:S(2)}, u32[]{:S(2)}) async-start(bf16[8,64,704]{2,1,0:T(8,128)(2,1)} %copy.341), calls=%async_computation.1 | async-start | bytes 1572864 | tf_op jit(solution)/shard_map/all_to_all | solution.py:993
  121.2 129.9 %reduce-scatter.6.cloned.1.call-start = ((), (), s32[]{:S(2)}) async-start(), calls=%async_computation.11 | async-start | bytes 4718592 | tf_op jit(solution)/shard_map/reduce_scatter | solution.py:971
  191.1 116.7 %all-gather.14.cloned.1.call-start = ((), (), s32[]{:S(2)}) async-start(), calls=%async_computation.13 | async-start | bytes 4718592 | tf_op jit(solution)/shard_map/all_gather | solution.py:968
  255.1 297.7 %reduce-scatter.8.cloned.1.call-start = ((), (), s32[]{:S(2)}) async-start(), calls=%async_computation.14 | async-start | bytes 4718592 | tf_op jit(solution)/shard_map/reduce_scatter | solution.py:971
  315.6 83.8 %collective-permute-start.21 = (bf16[4,72,2048]{2,1,0:T(8,128)(2,1)}, bf16[4,72,2048]{2,1,0:T(8,128)(2,1)}, u32[]{:S(2)}, u32[]{:S(2)}) collective-permute-start(bf16[4,72,2048]{2,1,0:T(8,128)(2,1)} %convolution_convert_fusion.10), channel_id=1, source_target_pairs={{0,24},{8,16},{16,8},{24,0},{1,25},{9,17},{17,9},{25,1},{2,26},{10... | collective-permute-start | bytes 3538952 | tf_op jit(solution)/shard_map/ppermute | solution.py:996
  404.8 64.4 %collective-permute-start.24 = (bf16[768,704]{0,1:T(8,128)(2,1)}, bf16[768,704]{0,1:T(8,128)(2,1)S(1)}, u32[]{:S(2)}, u32[]{:S(2)}) collective-permute-start(bf16[768,704]{0,1:T(8,128)(2,1)} %copy.353), channel_id=1, source_target_pairs={{0,24},{8,16},{16,8},{24,0},{1,25},{9,17},{17,9},{25,1},{2,26},{10... | collective-permute-start | bytes 3244040 | tf_op jit(solution)/shard_map/ppermute | solution.py:996
  406.2 62.9 %collective-permute-start.23 = (bf16[768,704]{0,1:T(8,128)(2,1)}, bf16[768,704]{0,1:T(8,128)(2,1)S(1)}, u32[]{:S(2)}, u32[]{:S(2)}) collective-permute-start(bf16[768,704]{0,1:T(8,128)(2,1)} %copy.352), channel_id=1, source_target_pairs={{0,16},{8,24},{16,0},{24,8},{1,17},{9,25},{17,1},{25,9},{2,18},{10... | collective-permute-start | bytes 3244040 | tf_op jit(solution)/shard_map/ppermute | solution.py:996
  406.6 62.6 %collective-permute-start.22 = (bf16[768,704]{0,1:T(8,128)(2,1)}, bf16[768,704]{0,1:T(8,128)(2,1)}, u32[]{:S(2)}, u32[]{:S(2)}) collective-permute-start(bf16[768,704]{0,1:T(8,128)(2,1)} %copy.351), channel_id=1, source_target_pairs={{0,8},{8,0},{16,24},{24,16},{1,9},{9,1},{17,25},{25,17},{2,10},{10... | collective-permute-start | bytes 3244040 | tf_op jit(solution)/shard_map/ppermute | solution.py:996
  503.7 122.5 %all-gather.16.cloned.1.call-start = ((), (), s32[]{:S(2)}) async-start(), calls=%async_computation.15 | async-start | bytes 4718592 | tf_op jit(solution)/shard_map/all_gather | solution.py:968
  557.2 128.3 %reduce-scatter.10.cloned.1.call-start = ((), (), s32[]{:S(2)}) async-start(), calls=%async_computation.16 | async-start | bytes 4718592 | tf_op jit(solution)/shard_map/reduce_scatter | solution.py:971
  636.5 123.7 %reduce-scatter.12.cloned.1.call-start = ((), (), s32[]{:S(2)}) async-start(), calls=%async_computation.17 | async-start | bytes 4718592 | tf_op jit(solution)/shard_map/reduce_scatter | solution.py:971
  685.5 106.6 %reduce-scatter.14.cloned.1.call-start = ((), (), s32[]{:S(2)}) async-start(), calls=%async_computation.18 | async-start | bytes 2949120 | tf_op jit(solution)/shard_map/reduce_scatter | solution.py:971
  705.3 170.1 %all-gather.18.cloned.1.call-start = ((), (), s32[]{:S(2)}) async-start(), calls=%async_computation.19 | async-start | bytes 5406720 | tf_op jit(solution)/shard_map/all_gather | solution.py:1366
  804.8 63.4 %all-to-all-start.3 = ((bf16[8,64,512]{2,1,0:T(8,128)(2,1)}), bf16[8,64,512]{2,1,0:T(8,128)(2,1)S(1)}, u32[]{:S(2)}, u32[]{:S(2)}) async-start(bf16[8,64,512]{2,1,0:T(8,128)(2,1)} %add_convert_fusion.4), calls=%async_computation.7 | async-start | bytes 1048576 | tf_op jit(solution)/shard_map/all_to_all | solution.py:993
  808.3 113.2 %all-gather.20.cloned.1.call-start = ((), (), s32[]{:S(2)}) async-start(), calls=%async_computation.20 | async-start | bytes 4341760 | tf_op jit(solution)/shard_map/all_gather | solution.py:1373
  818.1 61.7 %collective-permute-start.45 = (bf16[2,512,1408]{2,1,0:T(8,128)(2,1)}, bf16[2,512,1408]{2,1,0:T(8,128)(2,1)}, u32[]{:S(2)}, u32[]{:S(2)}) collective-permute-start(bf16[2,512,1408]{2,1,0:T(8,128)(2,1)} %pad_maximum_fusion), channel_id=1, source_target_pairs={{0,1},{1,0},{2,3},{3,2},{4,5},{5,4},{6,7},{7,6},{8,9},{9,8},{10,11... | collective-permute-start | bytes 8650760 | tf_op jit(solution)/shard_map/ppermute | solution.py:977
  (180 other events, 3076.3 us)
Sparse Core Ops, SparseCore 0:
  11.9 46.6 all-gather.9
  60.2 46.0 all-gather.7
  107.9 62.5 all-gather.11
  191.2 49.7 reduce-scatter.5
  255.2 45.1 all-gather.13
  503.8 48.8 reduce-scatter.7
  557.3 48.2 all-gather.15
  636.6 48.8 reduce-scatter.9
  688.4 60.7 reduce-scatter.11
  751.9 40.1 reduce-scatter.13
  794.5 76.1 all-gather.17
  875.5 46.0 all-gather.19
